TPU v7x, 128 devices: a whole 4x4x4 slice. The times are simulated.
128 devices in a mesh: dp: 32 (over y, x, core), fsdp: 4 (over z).
Axes of the slice: x: 4, y: 4, z: 4, core: 2. Of those that a mesh axis runs over, the one named last changes fastest.
Arguments:
- memory: bfloat16 [16384, 4096], P('dp'), may hold values from -6 to 6
- key_weight: bfloat16 [4096, 2048], P('dp', 'fsdp'), may hold values from -0.09375 to 0.09375
- value_weight: bfloat16 [4096, 2048], P('dp', 'fsdp'), may hold values from -0.09375 to 0.09375
- query: bfloat16 [16384, 2048], P('dp', 'fsdp')
- grad_context: bfloat16 [16384, 2048], P('dp', 'fsdp')
- target_segment: int32 [32, 512], P('dp'), may hold values from 0 to 31, never falling along the last dimension, each value on 1 to 32 neighbouring positions
- memory_segment: int32 [32, 512], P('dp'), may hold values from 0 to 31, never falling along the last dimension, each value on 1 to 128 neighbouring positions
- example_pack: int32 [32, 32], replicated, may hold values from 0 to 31, as said below
- example_slot: int32 [32, 32], replicated, may hold values from 0 to 31, as said below
Outputs:
- context: bfloat16 [16384, 2048], P('dp', 'fsdp')
- grad_query: bfloat16 [16384, 2048], P('dp', 'fsdp')
- grad_key_weight: float32 [4096, 2048], P('dp', 'fsdp')
- grad_value_weight: float32 [4096, 2048], P('dp', 'fsdp')
- grad_memory: bfloat16 [16384, 4096], P(('dp', 'fsdp'))
Inputs may be any that keep to these rules, and one draw needn't show every extreme that they name: `target_segment`: rows of each target pack are ordered by example; every one of the 32 examples has 1 to 32 decoder rows, and some example has exactly 32. `memory_segment`: rows of each input pack are ordered by segment; every one of the 32 segments has 1 to 128 memory rows, and some segment has exactly 128. `example_pack`: the 32 examples of one target pack have their memory in 32 different input packs, and every input pack holds the memory of exactly 32 examples. `example_slot`: the examples whose memory lies in one input pack carry the segment numbers 0 to 31 of that pack, each once.
All inputs are finite; a program needn't handle non-finite values.
Results may differ from a plain program's by a relative error of at most 0.017.
Values may be sent and summed in bfloat16 or wider, within the bound.
No kernel may reach another device: no remote copies, remote signals or barrier semaphores. Data moves between devices by JAX's collectives and lax.ppermute only.
A program may use at most 128 MiB of HBM per device.

v0:
```python
import jax
import jax.numpy as jnp
from jax import lax
from jax.sharding import PartitionSpec as P

HD = 256


SCORE_SCALE = 0.0625
MASKED_SCORE = -1e30


def lookup(table, indices):
    positions = jnp.arange(table.shape[0], dtype=jnp.int32)
    return jnp.sum(jnp.where(indices[..., None] == positions, table, 0), axis=-1)


def slot_layout(segment, my_packs, peer_count, depth):
    example_ids = jnp.arange(my_packs.shape[0], dtype=jnp.int32)
    member = (segment[None, :] == example_ids[:, None]).astype(jnp.int32)
    counts = jnp.sum(member, axis=1)
    starts = jnp.cumsum(counts) - counts
    peer_ids = jnp.arange(peer_count, dtype=jnp.int32)
    matched = my_packs[None, :] == peer_ids[:, None]
    chosen = jnp.sum(jnp.where(matched, example_ids[None, :], 0), axis=1)
    present = jnp.any(matched, axis=1)
    offsets = jnp.arange(depth, dtype=jnp.int32)
    live = present[:, None] & (offsets[None, :] < lookup(counts, chosen)[:, None])
    source = jnp.where(live, lookup(starts, chosen)[:, None] + offsets[None, :], 0)
    positions = jnp.arange(segment.shape[0], dtype=jnp.int32)
    target_slot = lookup(my_packs, segment) * depth + positions - lookup(starts, segment)
    return (source, live, target_slot)


def to_slots(row_data, source, live):
    peer_count, depth = source.shape
    taken = jnp.take(row_data, source.reshape(-1), axis=0).reshape(
        peer_count, depth, row_data.shape[1]
    )
    return jnp.where(live[..., None], taken, jnp.zeros_like(taken))


def from_slots(slot_data, target_slot):
    flat_data = slot_data.reshape(-1, slot_data.shape[2])
    return jnp.take(flat_data, target_slot, axis=0)


def pair_scores(left, key_set):
    return jnp.einsum("trhd,khd->thrk", left, key_set, preferred_element_type=jnp.float32)


def apply_weights(weights, value_set):
    return jnp.einsum("thrk,khd->trhd", weights, value_set, preferred_element_type=jnp.float32)


def spread_back(weights, right):
    return jnp.einsum("thrk,trhd->khd", weights, right, preferred_element_type=jnp.float32)


def softmax_weights(query_set, key_set, valid):
    scores = pair_scores(query_set, key_set) * SCORE_SCALE
    scores = jnp.where(valid[:, None, None, :], scores, MASKED_SCORE)
    row_top = jnp.max(scores, axis=-1, keepdims=True)
    raised = jnp.exp(scores - row_top)
    return raised / jnp.sum(raised, axis=-1, keepdims=True)


def per_device(
    memory,
    key_weight,
    value_weight,
    query,
    grad_context,
    target_segment,
    memory_segment,
    example_pack,
    example_slot,
):
    peer_count = lax.axis_size("dp")
    my_index = lax.axis_index("dp")
    width = key_weight.shape[1]
    heads = width // HD
    row_count = memory.shape[0]
    depth = 2 * query.shape[0] // peer_count
    stacked = jnp.stack((key_weight, value_weight), axis=1)
    piece = lax.all_gather(stacked, "dp", axis=0, tiled=True)
    columns = memory
    projected = jnp.dot(
        columns, piece.reshape(piece.shape[0], 2 * width), preferred_element_type=jnp.float32
    )
    key_rows = projected[:, :width].astype(jnp.bfloat16).reshape(row_count, heads, HD)
    value_rows = projected[:, width:].astype(jnp.bfloat16).reshape(row_count, heads, HD)
    mem_segment = memory_segment[0]
    owned = example_pack == my_index
    wanted = jnp.where(
        jnp.any(owned, axis=1), jnp.sum(jnp.where(owned, example_slot, 0), axis=1), -1
    )
    valid = mem_segment[None, :] == wanted[:, None]
    my_packs = lax.dynamic_index_in_dim(example_pack, my_index, 0, keepdims=False)
    source, live, target_slot = slot_layout(target_segment[0], my_packs, peer_count, depth)
    outgoing = to_slots(query, source, live)
    piece = lax.all_to_all(outgoing, "dp", split_axis=0, concat_axis=0, tiled=True)
    query_set = piece.reshape(peer_count, piece.shape[1], heads, HD)
    weights = softmax_weights(query_set, key_rows, valid).astype(jnp.bfloat16)
    mixed = apply_weights(weights, value_rows)
    answers = mixed.astype(jnp.bfloat16).reshape(peer_count, piece.shape[1], width)
    arrived = piece
    returned = lax.all_to_all(answers, "dp", split_axis=0, concat_axis=0, tiled=True)
    context = from_slots(returned, target_slot)
    grad_outgoing = to_slots(grad_context, source, live)
    grad_arrived = lax.all_to_all(grad_outgoing, "dp", split_axis=0, concat_axis=0, tiled=True)
    query_set = arrived.reshape(peer_count, depth, heads, HD)
    grad_set = grad_arrived.reshape(peer_count, depth, heads, HD)
    probability = softmax_weights(query_set, key_rows, valid)
    rounded = probability.astype(jnp.bfloat16)
    grad_prob = pair_scores(grad_set, value_rows)
    row_delta = jnp.sum(probability * grad_prob, axis=-1, keepdims=True)
    grad_scores = (probability * (grad_prob - row_delta) * SCORE_SCALE).astype(jnp.bfloat16)
    slot_grad = (
        apply_weights(grad_scores, key_rows).astype(jnp.bfloat16).reshape(peer_count, depth, width)
    )
    grad_returned = lax.all_to_all(slot_grad, "dp", split_axis=0, concat_axis=0, tiled=True)
    grad_query = from_slots(grad_returned, target_slot)
    grad_keys = spread_back(grad_scores, query_set)
    grad_values = spread_back(rounded, grad_set)
    grad_kv = jnp.concatenate(
        [
            grad_keys.astype(jnp.bfloat16).reshape(row_count, width),
            grad_values.astype(jnp.bfloat16).reshape(row_count, width),
        ],
        axis=1,
    )
    columns = memory
    weight_grads = lax.psum_scatter(
        lax.dot_general(
            columns, grad_kv, (((0,), (0,)), ((), ())), preferred_element_type=jnp.float32
        ).astype(jnp.bfloat16),
        "dp",
        scatter_dimension=0,
        tiled=True,
    ).astype(jnp.float32)
    piece = lax.all_gather(stacked, "dp", axis=0, tiled=True)
    flat_piece = piece.reshape(piece.shape[0], 2 * width)
    partial_sums = lax.dot_general(
        grad_kv, flat_piece, (((1,), (1,)), ((), ())), preferred_element_type=jnp.float32
    )
    grad_memory = lax.psum_scatter(partial_sums, "fsdp", scatter_dimension=0, tiled=True)
    return (
        context,
        grad_query,
        weight_grads[:, :width],
        weight_grads[:, width:],
        grad_memory.astype(jnp.bfloat16),
    )


def solution(mesh):
    placed = (
        P("dp", None),
        P("dp", "fsdp"),
        P("dp", "fsdp"),
        P("dp", "fsdp"),
        P("dp", "fsdp"),
        P("dp", None),
        P("dp", None),
        P(),
        P(),
    )
    return jax.shard_map(
        per_device,
        mesh=mesh,
        in_specs=placed,
        out_specs=(
            P("dp", "fsdp"),
            P("dp", "fsdp"),
            P("dp", "fsdp"),
            P("dp", "fsdp"),
            P(("dp", "fsdp"), None),
        ),
        check_vma=False,
    )
```

profile of v0, /device:TPU:0, one launch (start us, length us, event | category | flops | bytes accessed | tf_op | source)
XLA Modules:
  0.0 346.6 jit_solution(4169301897632804495)
XLA Ops:
  12.5 4.0 %gather_fusion.2 = bf16[1024,512]{1,0:T(8,128)(2,1)S(1)} fusion(bf16[512,512]{1,0:T(8,128)(2,1)S(1)} %copy-done, s32[1024]{0:T(1024)S(1)} %fusion.35), kind=kCustom, calls=%fused_computation.2.clone | custom fusion | bytes 2101248 | tf_op jit(solution)/shard_map/jit(_take)/gather | solution.py:37
  16.5 4.0 %gather_fusion = bf16[1024,512]{1,0:T(8,128)(2,1)S(1)} fusion(bf16[512,512]{1,0:T(8,128)(2,1)S(1)} %copy-done.2, s32[1024]{0:T(1024)S(1)} %fusion.35), kind=kCustom, calls=%fused_computation.clone | custom fusion | bytes 2101248 | tf_op jit(solution)/shard_map/jit(_take)/gather | solution.py:37
  22.0 25.2 %all_to_all.20 = bf16[32,32,512]{2,1,0:T(8,128)(2,1)S(1)} all-to-all(bf16[32,32,512]{2,1,0:T(8,128)(2,1)S(1)} %get-tuple-element.40), channel_id=1, replica_groups=mesh['dp'=32,'fsdp'=4] {'dp'}, dimensions={0} | all-to-all | bytes 2097152 | tf_op jit(solution)/shard_map/all_to_all | solution.py:102
  47.3 4.3 %all-to-all-start.2 = ((bf16[32,32,512]{2,1,0:T(8,128)(2,1)}), bf16[32,32,512]{2,1,0:T(8,128)(2,1)S(1)}, u32[]{:S(2)}, u32[]{:S(2)}) async-start(bf16[32,32,512]{2,1,0:T(8,128)(2,1)} %get-tuple-element.39), calls=%async_computation.2 | async-start | bytes 2097152 | tf_op jit(solution)/shard_map/all_to_all | solution.py:111
  53.3 21.2 %all-to-all-done.2 = bf16[32,32,512]{2,1,0:T(8,128)(2,1)S(1)} async-done(((bf16[32,32,512]{2,1,0:T(8,128)(2,1)}), bf16[32,32,512]{2,1,0:T(8,128)(2,1)S(1)}, u32[]{:S(2)}, u32[]{:S(2)}) %all-to-all-start.2) | async-done | bytes 1048608 | tf_op jit(solution)/shard_map/all_to_all | solution.py:111
  75.7 16.1 %all-gather.2.cloned.1.call-done = bf16[4096,2,512]{0,2,1:T(8,128)(2,1)} async-done(((bf16[128,2,512]{0,2,1:T(8,128)(2,1)}), bf16[4096,2,512]{0,2,1:T(8,128)(2,1)}) %all-gather.2.cloned.1.call-update) | async-done | bytes 8388624 | tf_op jit(solution)/shard_map/all_gather | solution.py:86
  91.7 9.2 %fusion.19 = bf16[512,1024]{0,1:T(8,128)(2,1)S(1)} fusion(bf16[4096,1024]{0,1:T(8,128)(2,1)} %bitcast.94, bf16[512,4096]{1,0:T(8,128)(2,1)} %param.13), kind=kOutput, calls=%fused_computation.23 | convolution fusion | flops 4295491584 | bytes 13631488 | tf_op jit(solution)/shard_map/dot_general | solution.py:88
  101.0 2.7 fusion.48
  104.4 6.1 %fusion.46 = (f32[32,2,32]{2,0,1:T(8,128)S(1)}, f32[32,2,32,512]{3,2,0,1:T(8,128)S(1)}) fusion(f32[2,512,32,32]{1,3,2,0:T(8,128)S(1)} %bitcast.100, pred[32,512]{1,0:T(8,128)(4,1)S(1)} %broadcast_compare_fusion), kind=kOutput, calls=%fused_computation.77 | output fusion | flops 6291967 | bytes 8413184 | tf_op jit(solution)/shard_map/sub | solution.py:64
  110.5 2.2 fusion.26
  112.6 15.8 %fusion.27 = bf16[2,256,512]{2,1,0:T(8,128)(2,1)S(1)} fusion(f32[32,2,32,512]{3,2,0,1:T(8,128)} %bitcast.98, bf16[32,4,2,8,256]{4,3,2,1,0:T(8,128)(2,1)S(1)} %bitcast.102, f32[32,2,32,512]{3,2,0,1:T(8,128)} %copy-done.10, f32[32,2,32]{2,0,1:T(8,128)S(1)} %get-tuple-element.45), kind=kOutput, calls=%fused_computation.28 | convolution fusion | flops 544475648 | bytes 9969664 | tf_op jit(solution)/shard_map/thrk,trhd->khd/dot_general | solution.py:57
  128.5 9.6 %convert_bitcast_fusion = bf16[4096,1024]{0,1:T(8,128)(2,1)} fusion(bf16[512,4096]{1,0:T(8,128)(2,1)} %param.13, bf16[512,512]{0,1:T(8,128)(2,1)S(1)} %bitcast.112, bf16[512,512]{0,1:T(8,128)(2,1)S(1)} %bitcast.114), kind=kOutput, calls=%fused_computation.6 | convolution fusion | flops 4301258752 | bytes 13631488 | tf_op jit(solution)/shard_map/dot_general | solution.py:135
  138.1 11.9 %copy.82 = bf16[4096,1024]{1,0:T(8,128)(2,1)} copy(bf16[4096,1024]{0,1:T(8,128)(2,1)} %convert_bitcast_fusion) | data formatting | bytes 16777216
  150.3 10.2 %fusion.32 = f32[512,4096]{1,0:T(8,128)} fusion(bf16[4096,1024]{0,1:T(8,128)(2,1)} %bitcast.95, bf16[512,512]{0,1:T(8,128)(2,1)S(1)} %bitcast.113, bf16[512,512]{0,1:T(8,128)(2,1)S(1)} %bitcast.115), kind=kOutput, calls=%fused_computation.38 | convolution fusion | flops 4297064448 | bytes 17825792 | tf_op jit(solution)/shard_map/dot_general | solution.py:144
  160.5 17.7 %fusion.20 = bf16[2,32,4,8,256]{4,3,2,1,0:T(8,128)(2,1)S(1)} fusion(bf16[512,2,256,1]{0,2,3,1:T(8,128)(2,1)S(1)} %bitcast.111, f32[32,2,32,512]{3,2,0,1:T(8,128)} %bitcast.99, f32[32,2,32,512]{3,2,0,1:T(8,128)} %copy-done.10, f32[32,2,32]{2,0,1:T(8,128)S(1)} %get-tuple-element.45), kind=kOutput, calls=%fused_computation.24 | convolution fusion | flops 544737792 | bytes 9969664 | tf_op jit(solution)/shard_map/thrk,khd->trhd/dot_general | solution.py:53
  179.3 5.5 %all-to-all-start.3 = ((bf16[32,32,512]{2,1,0:T(8,128)(2,1)}), bf16[32,32,512]{2,1,0:T(8,128)(2,1)S(1)}, u32[]{:S(2)}, u32[]{:S(2)}) async-start(bf16[32,32,512]{2,1,0:T(8,128)(2,1)} %bitcast.54), calls=%async_computation.3 | async-start | bytes 2097152 | tf_op jit(solution)/shard_map/all_to_all | solution.py:122
  184.9 3.2 fusion.18
  189.2 13.1 %all-to-all-done.3 = bf16[32,32,512]{2,1,0:T(8,128)(2,1)S(1)} async-done(((bf16[32,32,512]{2,1,0:T(8,128)(2,1)}), bf16[32,32,512]{2,1,0:T(8,128)(2,1)S(1)}, u32[]{:S(2)}, u32[]{:S(2)}) %all-to-all-start.3) | async-done | bytes 1048608 | tf_op jit(solution)/shard_map/all_to_all | solution.py:122
  202.2 3.9 %all-to-all-start.1 = ((bf16[32,32,512]{2,1,0:T(8,128)(2,1)}), bf16[32,32,512]{2,1,0:T(8,128)(2,1)S(1)}, u32[]{:S(2)}, u32[]{:S(2)}) async-start(bf16[32,32,512]{2,1,0:T(8,128)(2,1)} %bitcast.105), calls=%async_computation.1 | async-start | bytes 2097152 | tf_op jit(solution)/shard_map/all_to_all | solution.py:108
  206.3 2.0 gather_fusion.3
  208.3 26.0 %all-to-all-done.1 = bf16[32,32,512]{2,1,0:T(8,128)(2,1)S(1)} async-done(((bf16[32,32,512]{2,1,0:T(8,128)(2,1)}), bf16[32,32,512]{2,1,0:T(8,128)(2,1)S(1)}, u32[]{:S(2)}, u32[]{:S(2)}) %all-to-all-start.1) | async-done | bytes 1048608 | tf_op jit(solution)/shard_map/all_to_all | solution.py:108
  237.4 17.2 %reduce-scatter.7.cloned.1.call-done = bf16[128,1024]{1,0:T(8,128)(2,1)} async-done(((bf16[4096,1024]{1,0:T(8,128)(2,1)}), bf16[128,1024]{1,0:T(8,128)(2,1)}) %reduce-scatter.7.cloned.1.call-update) | async-done | bytes 262160
  257.4 79.9 %reduce-scatter.5.cloned.1.call-done = f32[128,4096]{1,0:T(8,128)} async-done(((f32[512,4096]{1,0:T(8,128)}), f32[128,4096]{1,0:T(8,128)}) %reduce-scatter.5.cloned.1.call-update) | async-done | bytes 2097168 | tf_op jit(solution)/shard_map/reduce_scatter | solution.py:147
  337.4 2.7 convert_element_type.62
  (66 shorter events, 18.9 us)
Async XLA Ops:
  7.2 5.3 %copy-start = (bf16[512,512]{1,0:T(8,128)(2,1)S(1)}, bf16[512,512]{1,0:T(8,128)(2,1)}, u32[]{:S(2)}) copy-start(bf16[512,512]{1,0:T(8,128)(2,1)} %param.17) | copy-start | bytes 1572868
  7.2 84.5 %all-gather.2.cloned.1.call-start = ((), (), s32[]{:S(2)}) async-start(), calls=%async_computation.6 | async-start | bytes 8650752 | tf_op jit(solution)/shard_map/all_gather | solution.py:86
  12.5 4.0 %copy-start.2 = (bf16[512,512]{1,0:T(8,128)(2,1)S(1)}, bf16[512,512]{1,0:T(8,128)(2,1)}, u32[]{:S(2)}) copy-start(bf16[512,512]{1,0:T(8,128)(2,1)} %param.16) | copy-start | bytes 1572868
  20.8 31.0 %copy-start.6 = (s32[32,32]{1,0:T(8,128)S(1)}, s32[32,32]{1,0:T(8,128)}, u32[]{:S(2)}) copy-start(s32[32,32]{1,0:T(8,128)} %param.20) | copy-start | bytes 12292
  20.8 31.0 %copy-start.7 = (s32[32,32]{1,0:T(8,128)S(1)}, s32[32,32]{1,0:T(8,128)}, u32[]{:S(2)}) copy-start(s32[32,32]{1,0:T(8,128)} %param.21) | copy-start | bytes 12292
  20.8 31.2 %copy-start.9 = (s32[1,512]{1,0:T(1,128)S(1)}, s32[1,512]{1,0:T(1,128)}, u32[]{:S(2)}) copy-start(s32[1,512]{1,0:T(1,128)} %param.19) | copy-start | bytes 6148
  47.3 27.3 %all-to-all-start.2 = ((bf16[32,32,512]{2,1,0:T(8,128)(2,1)}), bf16[32,32,512]{2,1,0:T(8,128)(2,1)S(1)}, u32[]{:S(2)}, u32[]{:S(2)}) async-start(bf16[32,32,512]{2,1,0:T(8,128)(2,1)} %get-tuple-element.39), calls=%async_computation.2 | async-start | bytes 2097152 | tf_op jit(solution)/shard_map/all_to_all | solution.py:111
  51.5 203.0 %reduce-scatter.7.cloned.1.call-start = ((), (), s32[]{:S(2)}) async-start(), calls=%async_computation.8 | async-start | bytes 8650752
  91.7 9.3 %copy-start.4 = (bf16[32,4,2,8,256]{4,3,1,0,2:T(8,128)(2,1)S(1)}, bf16[32,4,2,8,256]{4,3,1,0,2:T(8,128)(2,1)}, u32[]{:S(2)}) copy-start(bf16[32,4,2,8,256]{4,3,1,0,2:T(8,128)(2,1)} %copy.92) | copy-start | bytes 3145732
  100.9 2.8 copy-start.3
  110.5 2.2 copy-start.10
  112.6 15.8 %copy-start.5 = (bf16[2,256,512]{2,1,0:T(8,128)(2,1)S(1)}, bf16[2,256,512]{2,1,0:T(8,128)(2,1)}, u32[]{:S(2)}) copy-start(bf16[2,256,512]{2,1,0:T(8,128)(2,1)} %fusion.26) | copy-start | bytes 1572868
  150.1 187.3 %reduce-scatter.5.cloned.1.call-start = ((), (), s32[]{:S(2)}) async-start(), calls=%async_computation.7 | async-start | bytes 10485760 | tf_op jit(solution)/shard_map/reduce_scatter | solution.py:147
  179.3 22.9 %all-to-all-start.3 = ((bf16[32,32,512]{2,1,0:T(8,128)(2,1)}), bf16[32,32,512]{2,1,0:T(8,128)(2,1)S(1)}, u32[]{:S(2)}, u32[]{:S(2)}) async-start(bf16[32,32,512]{2,1,0:T(8,128)(2,1)} %bitcast.54), calls=%async_computation.3 | async-start | bytes 2097152 | tf_op jit(solution)/shard_map/all_to_all | solution.py:122
  188.1 18.1 %copy-start.8 = (s32[1,512]{1,0:T(1,128)S(1)}, s32[1,512]{1,0:T(1,128)}, u32[]{:S(2)}) copy-start(s32[1,512]{1,0:T(1,128)} %param.18) | copy-start | bytes 6148
  202.2 32.1 %all-to-all-start.1 = ((bf16[32,32,512]{2,1,0:T(8,128)(2,1)}), bf16[32,32,512]{2,1,0:T(8,128)(2,1)S(1)}, u32[]{:S(2)}, u32[]{:S(2)}) async-start(bf16[32,32,512]{2,1,0:T(8,128)(2,1)} %bitcast.105), calls=%async_computation.1 | async-start | bytes 2097152 | tf_op jit(solution)/shard_map/all_to_all | solution.py:108
  234.3 105.8 %copy-start.1 = (bf16[512,512]{1,0:T(8,128)(2,1)S(1)}, bf16[512,512]{1,0:T(8,128)(2,1)}, u32[]{:S(2)}) copy-start(bf16[512,512]{1,0:T(8,128)(2,1)} %param.17) | copy-start | bytes 1572868
Sparse Core Ops, SparseCore 0:
  10.8 80.8 all-gather.1
  150.2 104.3 reduce-scatter.6
  257.2 80.1 reduce-scatter.4
where the time goes:
time: 348 us; the launch traced here: 347 us
  waiting for transfers between devices  173 us (50%)
  matrix products  71.3 us (20%)
  local copies, waits for them, and re-layouts  34.2 us (10%)
  blocking collectives  25.2 us (7%)
  starting transfers between devices  14.3 us (4%)
  other arithmetic  14.1 us (4%)
  between operations  14.1 us (4%)
    reduce_scatter x1, waiting for transfers between devices, per_device(): lax.psum_scatter(partial_sums, 'fsdp', scatter_dimension=0, tiled=True)  79.9 us
    all_to_all x1, waiting for transfers between devices, per_device(): lax.all_to_all(answers, 'dp', split_axis=0, concat_axis=0, tiled=True)  26 us
    all_to_all x1, blocking collectives, per_device(): lax.all_to_all(outgoing, 'dp', split_axis=0, concat_axis=0, tiled=True)  25.2 us
    all_to_all x1, waiting for transfers between devices, per_device(): lax.all_to_all(grad_outgoing, 'dp', split_axis=0, concat_axis=0, tiled=True)  21.2 us
    dot_general x2, matrix products, apply_weights(): jnp.einsum('thrk,khd->trhd', weights, value_set, preferred_element_type=j...  20.9 us
    dot_general x2, matrix products, spread_back(): jnp.einsum('thrk,trhd->khd', weights, right, preferred_element_type=jnp.f...  18 us
    unnamed x4, waiting for transfers between devices  17.2 us
    unnamed x28, local copies, waits for them, and re-layouts  16.9 us
  transfers between devices with their start and end apart: 6, of which 6 were waited for; matrix products, arithmetic and copies ran while one was open for 16% of the time, Pallas kernels for 0%

commit v1 on v0

v1 whole, which is shorter than its diff:
```python
import jax
import jax.numpy as jnp
from jax import lax
from jax.experimental import pallas as pl
from jax.experimental.pallas import tpu as pltpu
from jax.sharding import PartitionSpec as P

HD = 256
PEERS = 32
DEPTH = 32
BLOCK_PEERS = 8


SCORE_SCALE = 0.0625
MASKED_SCORE = -1e30


def dot(left, right, left_dim, right_dim):
    return lax.dot_general(
        left, right, (((left_dim,), (right_dim,)), ((), ())), preferred_element_type=jnp.float32
    )


def target_slots(segment, my_packs):
    rows = segment.shape[0]
    earlier = jnp.sum((segment[None, :] < segment[:, None]).astype(jnp.int32), axis=1)
    example_ids = jnp.arange(my_packs.shape[0], dtype=jnp.int32)
    pack = jnp.sum(
        jnp.where(segment[:, None] == example_ids[None, :], my_packs[None, :], 0), axis=1
    )
    return pack * DEPTH + jnp.arange(rows, dtype=jnp.int32) - earlier


def pack_body(slot_ref, query_ref, grad_ref, out_ref):
    block = pl.program_id(0)
    rows = BLOCK_PEERS * DEPTH
    positions = block * rows + lax.broadcasted_iota(jnp.int32, (rows, slot_ref.shape[1]), 0)
    chosen = jnp.where(positions == slot_ref[...], 1.0, 0.0).astype(jnp.bfloat16)
    for part, source in enumerate((query_ref, grad_ref)):
        taken = dot(chosen, source[...], 1, 0).astype(jnp.bfloat16)
        out_ref[:, part] = taken.reshape(BLOCK_PEERS, DEPTH, taken.shape[1])


def pack_slots(slots, query, grad_context):
    rows, width = query.shape
    return pl.pallas_call(
        pack_body,
        grid=(PEERS // BLOCK_PEERS,),
        in_specs=[
            pl.BlockSpec((1, rows), lambda i: (0, 0)),
            pl.BlockSpec((rows, width), lambda i: (0, 0)),
            pl.BlockSpec((rows, width), lambda i: (0, 0)),
        ],
        out_specs=pl.BlockSpec((BLOCK_PEERS, 2, DEPTH, width), lambda i: (i, 0, 0, 0)),
        out_shape=jax.ShapeDtypeStruct((PEERS, 2, DEPTH, width), jnp.bfloat16),
        name="pack_slots",
    )(slots.reshape(1, rows), query, grad_context)


def unpack_body(slot_ref, in_ref, context_ref, grad_ref):
    slots = PEERS * DEPTH
    positions = lax.broadcasted_iota(jnp.int32, (slot_ref.shape[0], slots), 1)
    chosen = jnp.where(positions == slot_ref[...], 1.0, 0.0).astype(jnp.bfloat16)
    for part, target in enumerate((context_ref, grad_ref)):
        data = in_ref[:, part].reshape(slots, in_ref.shape[3])
        target[...] = dot(chosen, data, 1, 0).astype(jnp.bfloat16)


def unpack_slots(slots, returned):
    rows = slots.shape[0]
    width = returned.shape[3]
    half = width // 2
    return pl.pallas_call(
        unpack_body,
        grid=(2,),
        in_specs=[
            pl.BlockSpec((rows, 1), lambda i: (0, 0)),
            pl.BlockSpec((PEERS, 2, DEPTH, half), lambda i: (0, 0, 0, i)),
        ],
        out_specs=[
            pl.BlockSpec((rows, half), lambda i: (0, i)),
            pl.BlockSpec((rows, half), lambda i: (0, i)),
        ],
        out_shape=[jax.ShapeDtypeStruct((rows, width), jnp.bfloat16)] * 2,
        name="unpack_slots",
    )(slots.reshape(rows, 1), returned)


def attend_body(
    wanted_ref, segment_ref, in_ref, key_ref, value_ref, out_ref, grad_kv_ref, key_sum, value_sum
):
    block = pl.program_id(1)
    rows = BLOCK_PEERS * DEPTH
    query = in_ref[:, 0].reshape(rows, HD)
    grad = in_ref[:, 1].reshape(rows, HD)
    keys = key_ref[...]
    values = value_ref[...]
    valid = wanted_ref[...] == segment_ref[...]
    scores = jnp.where(valid, dot(query, keys, 1, 1) * SCORE_SCALE, MASKED_SCORE)
    grad_prob = dot(grad, values, 1, 1)
    raised = jnp.exp(scores - jnp.max(scores, axis=1, keepdims=True))
    probability = raised / jnp.sum(raised, axis=1, keepdims=True)
    rounded = probability.astype(jnp.bfloat16)
    row_delta = jnp.sum(probability * grad_prob, axis=1, keepdims=True)
    grad_scores = (probability * (grad_prob - row_delta) * SCORE_SCALE).astype(jnp.bfloat16)
    context = dot(rounded, values, 1, 0).astype(jnp.bfloat16)
    out_ref[:, 0] = context.reshape(BLOCK_PEERS, DEPTH, HD)
    grad_query = dot(grad_scores, keys, 1, 0).astype(jnp.bfloat16)
    out_ref[:, 1] = grad_query.reshape(BLOCK_PEERS, DEPTH, HD)
    key_term = dot(grad_scores, query, 0, 0)
    value_term = dot(rounded, grad, 0, 0)

    @pl.when(block == 0)
    def _():
        key_sum[...] = key_term
        value_sum[...] = value_term

    @pl.when(block > 0)
    def _():
        key_sum[...] += key_term
        value_sum[...] += value_term

    @pl.when(block == pl.num_programs(1) - 1)
    def _():
        grad_kv_ref[0] = key_sum[...].astype(jnp.bfloat16)
        grad_kv_ref[1] = value_sum[...].astype(jnp.bfloat16)


def attend(wanted, segment, arrived, kv):
    memory_rows = segment.shape[0]
    width = arrived.shape[3]
    heads = width // HD
    rows = BLOCK_PEERS * DEPTH
    wanted_rows = jnp.broadcast_to(wanted[:, None], (PEERS, DEPTH)).reshape(PEERS * DEPTH, 1)
    return pl.pallas_call(
        attend_body,
        grid=(heads, PEERS // BLOCK_PEERS),
        in_specs=[
            pl.BlockSpec((rows, 1), lambda h, i: (i, 0)),
            pl.BlockSpec((1, memory_rows), lambda h, i: (0, 0)),
            pl.BlockSpec((BLOCK_PEERS, 2, DEPTH, HD), lambda h, i: (i, 0, 0, h)),
            pl.BlockSpec((memory_rows, HD), lambda h, i: (0, h)),
            pl.BlockSpec((memory_rows, HD), lambda h, i: (0, heads + h)),
        ],
        out_specs=[
            pl.BlockSpec((BLOCK_PEERS, 2, DEPTH, HD), lambda h, i: (i, 0, 0, h)),
            pl.BlockSpec((2, memory_rows, HD), lambda h, i: (0, 0, h)),
        ],
        out_shape=[
            jax.ShapeDtypeStruct(arrived.shape, jnp.bfloat16),
            jax.ShapeDtypeStruct((2, memory_rows, width), jnp.bfloat16),
        ],
        scratch_shapes=[pltpu.VMEM((memory_rows, HD), jnp.float32)] * 2,
        name="attend",
    )(wanted_rows, segment.reshape(1, memory_rows), arrived, kv, kv)


def per_device(
    memory,
    key_weight,
    value_weight,
    query,
    grad_context,
    target_segment,
    memory_segment,
    example_pack,
    example_slot,
):
    my_index = lax.axis_index("dp")
    width = key_weight.shape[1]
    stacked = jnp.concatenate((key_weight, value_weight), axis=1)
    weights = lax.all_gather(stacked, "dp", axis=0, tiled=True)
    my_packs = lax.dynamic_index_in_dim(example_pack, my_index, 0, keepdims=False)
    slots = target_slots(target_segment[0], my_packs)
    outgoing = pack_slots(slots, query, grad_context)
    arrived = lax.all_to_all(outgoing, "dp", split_axis=0, concat_axis=0, tiled=True)
    owned = example_pack == my_index
    wanted = jnp.where(
        jnp.any(owned, axis=1), jnp.sum(jnp.where(owned, example_slot, 0), axis=1), -1
    )
    kv = dot(memory, weights, 1, 0).astype(jnp.bfloat16)
    answers, grad_kv = attend(wanted, memory_segment[0], arrived, kv)
    grad_kv = jnp.concatenate((grad_kv[0], grad_kv[1]), axis=1)
    weight_terms = dot(memory, grad_kv, 0, 0).astype(jnp.bfloat16)
    weight_grads = lax.psum_scatter(
        weight_terms, "dp", scatter_dimension=0, tiled=True
    ).astype(jnp.float32)
    returned = lax.all_to_all(answers, "dp", split_axis=0, concat_axis=0, tiled=True)
    context, grad_query = unpack_slots(slots, returned)
    partial_sums = dot(grad_kv, weights, 1, 1).astype(jnp.bfloat16)
    grad_memory = lax.psum_scatter(partial_sums, "fsdp", scatter_dimension=0, tiled=True)
    return (
        context,
        grad_query,
        weight_grads[:, :width],
        weight_grads[:, width:],
        grad_memory,
    )


def solution(mesh):
    placed = (
        P("dp", None),
        P("dp", "fsdp"),
        P("dp", "fsdp"),
        P("dp", "fsdp"),
        P("dp", "fsdp"),
        P("dp", None),
        P("dp", None),
        P(),
        P(),
    )
    return jax.shard_map(
        per_device,
        mesh=mesh,
        in_specs=placed,
        out_specs=(
            P("dp", "fsdp"),
            P("dp", "fsdp"),
            P("dp", "fsdp"),
            P("dp", "fsdp"),
            P(("dp", "fsdp"), None),
        ),
        check_vma=False,
    )
```

time: 348 us -> 279 us (0.80)
  matrix products: 71.3 us -> 28.6 us
  blocking collectives: 25.2 us -> 0 us
  Pallas kernels: 0 us -> 18.9 us
  local copies, waits for them, and re-layouts: 34.2 us -> 21.2 us
  other arithmetic: 14.1 us -> 5.04 us
    all_gather x1, waiting for transfers between devices: 16.1 us -> 58.2 us  [per_device(): weights = lax.all_gather(stacked, 'dp', axis=0, tiled=True)]
    dot_general x7 -> x3, matrix products: 67.9 us -> 28.6 us  [dot(): lax.dot_general(left, right, (((left_dim,), (right_dim,)), ((), ())), pre...]
    all_to_all x2 -> x1, waiting for transfers between devices: 34.3 us -> 0.01 us  [per_device(): lax.all_to_all(outgoing, 'dp', split_axis=0, concat_axis=0, tiled=True)]
    reduce_scatter x1, waiting for transfers between devices: 79.9 us -> 46.7 us  [per_device(): lax.psum_scatter(partial_sums, 'fsdp', scatter_dimension=0, tiled=True)]
    unnamed x4, waiting for transfers between devices: 17.2 us -> 42.5 us
    all_to_all x1 -> x0, blocking collectives: 25.2 us -> none  [per_device(): lax.all_to_all(outgoing, 'dp', split_axis=0, concat_axis=0, tiled=True)]
    pallas_call x0 -> x3, Pallas kernels: none -> 18.9 us  [the longest x1 11.2 us: attend(): pl.pallas_call(attend_body, grid=(heads, PEERS // BLOCK_PEERS), in_specs=...]
    gather x4 -> x0, local copies, waits for them, and re-layouts: 11.9 us -> none  [the longest x2 7.93 us: to_slots(): jnp.take(row_data, source.reshape(-1), axis=0)]
  transfers between devices with their start and end apart: 6 -> 5, of which waited for: 6 -> 4; matrix products, arithmetic and copies ran while one was open for 16% -> 10% of each run, Pallas kernels for 0% -> 3%
where the time goes in v1:
time: 279 us; the launch traced here: 277 us
  waiting for transfers between devices  176 us (63%)
  matrix products  28.6 us (10%)
  local copies, waits for them, and re-layouts  21.2 us (8%)
  Pallas kernels  18.9 us (7%)
  between operations  13.9 us (5%)
  starting transfers between devices  13 us (5%)
  other arithmetic  5.04 us (2%)
    all_gather x1, waiting for transfers between devices, per_device(): weights = lax.all_gather(stacked, 'dp', axis=0, tiled=True)  58.2 us
    reduce_scatter x1, waiting for transfers between devices, per_device(): lax.psum_scatter(partial_sums, 'fsdp', scatter_dimension=0, tiled=True)  46.7 us
    unnamed x4, waiting for transfers between devices  42.5 us
    all_to_all x1, waiting for transfers between devices, per_device(): lax.all_to_all(answers, 'dp', split_axis=0, concat_axis=0, tiled=True)  28.9 us
    dot_general x3, matrix products, dot(): lax.dot_general(left, right, (((left_dim,), (right_dim,)), ((), ())), pre...  28.6 us
    unnamed x12, local copies, waits for them, and re-layouts  17.4 us
    pallas_call x1, Pallas kernels, attend(): pl.pallas_call(attend_body, grid=(heads, PEERS // BLOCK_PEERS), in_specs=...  11.2 us
    all_to_all x1, starting transfers between devices, per_device(): lax.all_to_all(outgoing, 'dp', split_axis=0, concat_axis=0, tiled=True)  7.4 us
  transfers between devices with their start and end apart: 5, of which 4 were waited for; matrix products, arithmetic and copies ran while one was open for 10% of the time, Pallas kernels for 3%

profile of v1, /device:TPU:0, one launch (start us, length us, event | category | flops | bytes accessed | tf_op | source)
XLA Modules:
  0.0 276.9 jit_solution(5091333146998626011)
XLA Ops:
  7.2 1.7 pad_maximum_fusion.3
  9.7 0.8 select_reduce_fusion
  10.4 1.0 convert_reduce_fusion
  12.0 4.2 %pack_slots.1 = bf16[32,2,32,512]{3,2,1,0:T(8,128)(2,1)} custom-call(s32[1,512]{1,0:T(1,128)} %add_subtract_fusion.slot_ref, bf16[512,512]{1,0:T(8,128)(2,1)} %query_ref.1, bf16[512,512]{1,0:T(8,128)(2,1)} %grad_ref.1), custom_call_target="tpu_custom_call" | custom-call | tf_op jit(solution)/shard_map/pack_slots/pallas_call | solution.py:46
  16.2 7.4 %all-to-all-start = ((bf16[32,2,32,512]{3,2,1,0:T(8,128)(2,1)}), bf16[32,2,32,512]{3,2,1,0:T(8,128)(2,1)S(1)}, u32[]{:S(2)}, u32[]{:S(2)}) async-start(bf16[32,2,32,512]{3,2,1,0:T(8,128)(2,1)} %pack_slots.1), calls=%async_computation | async-start | bytes 4194304 | tf_op jit(solution)/shard_map/all_to_all | solution.py:176
  24.0 1.3 reshape.68.wanted_ref
  25.3 58.2 %all-gather.2.cloned.1.call-done = bf16[4096,1024]{1,0:T(8,128)(2,1)} async-done(((bf16[128,1024]{1,0:T(8,128)(2,1)}), bf16[4096,1024]{1,0:T(8,128)(2,1)}) %all-gather.2.cloned.1.call-update) | async-done | bytes 8388624 | tf_op jit(solution)/shard_map/all_gather | solution.py:172
  83.5 10.1 %fusion.key_ref.value_ref = bf16[512,1024]{1,0:T(8,128)(2,1)} fusion(bf16[512,4096]{1,0:T(8,128)(2,1)} %param.9, bf16[4096,1024]{1,0:T(8,128)(2,1)} %all-gather.2.cloned.1.call-done), kind=kOutput, calls=%fused_computation.3 | convolution fusion | flops 4295491584 | bytes 13631488 | tf_op jit(solution)/shard_map/dot_general | solution.py:19
  93.6 1.3 copy-done
  95.0 11.2 %attend.1 = (bf16[32,2,32,512]{3,2,1,0:T(8,128)(2,1)}, bf16[2,512,512]{2,1,0:T(8,128)(2,1)}) custom-call(s32[1024,1]{1,0:T(8,128)} %reshape.68.wanted_ref, s32[1,512]{1,0:T(1,128)} %segment_ref.1, bf16[32,2,32,512]{3,2,1,0:T(8,128)(2,1)} %copy-done, bf16[512,1024]{1,0:T(8,128)(2,1)} %fusion.key_ref.value_ref, bf16[512,1024]{1,0:T(8,128)(2,1)} %fusion.key_ref.value_ref), custom_call_target="tpu_custom_call" | custom-call | tf_op jit(solution)/shard_map/attend/pallas_call | solution.py:135
  106.1 1.3 slice_bitcast_fusion.1
  107.4 9.0 %convert_bitcast_fusion = bf16[4096,1024]{0,1:T(8,128)(2,1)} fusion(bf16[512,4096]{1,0:T(8,128)(2,1)} %param.9, bf16[512,512]{1,0:T(8,128)(2,1)S(1)} %get-tuple-element.41, bf16[512,512]{1,0:T(8,128)(2,1)S(1)} %get-tuple-element.40), kind=kOutput, calls=%fused_computation | convolution fusion | flops 4301258752 | bytes 13631488 | tf_op jit(solution)/shard_map/dot_general | solution.py:19
  116.4 12.0 %copy.42 = bf16[4096,1024]{1,0:T(8,128)(2,1)} copy(bf16[4096,1024]{0,1:T(8,128)(2,1)} %convert_bitcast_fusion) | data formatting | bytes 16777216
  128.4 9.5 %convolution_convert_fusion = bf16[512,4096]{1,0:T(8,128)(2,1)} fusion(bf16[4096,1024]{1,0:T(8,128)(2,1)} %all-gather.2.cloned.1.call-done, bf16[512,512]{1,0:T(8,128)(2,1)S(1)} %get-tuple-element.41, bf16[512,512]{1,0:T(8,128)(2,1)S(1)} %get-tuple-element.40), kind=kOutput, calls=%fused_computation.1 | convolution fusion | flops 4299161600 | bytes 13631488 | tf_op jit(solution)/shard_map/dot_general | solution.py:19
  137.9 5.5 %all-to-all-start.1 = ((bf16[32,2,32,512]{3,2,1,0:T(8,128)(2,1)}), bf16[32,2,32,512]{3,2,1,0:T(8,128)(2,1)S(1)}, u32[]{:S(2)}, u32[]{:S(2)}) async-start(bf16[32,2,32,512]{3,2,1,0:T(8,128)(2,1)} %get-tuple-element.9), calls=%async_computation.1 | async-start | bytes 4194304 | tf_op jit(solution)/shard_map/all_to_all | solution.py:188
  143.7 0.7 sub.19.slot_ref
  144.5 28.9 %all-to-all-done.1.in_ref = bf16[32,2,32,512]{3,2,1,0:T(8,128)(2,1)S(1)} async-done(((bf16[32,2,32,512]{3,2,1,0:T(8,128)(2,1)}), bf16[32,2,32,512]{3,2,1,0:T(8,128)(2,1)S(1)}, u32[]{:S(2)}, u32[]{:S(2)}) %all-to-all-start.1) | async-done | bytes 2097184 | tf_op jit(solution)/shard_map/all_to_all | solution.py:188
  173.4 1.3 copy-done.1
  174.7 3.6 %unpack_slots.1 = (bf16[512,512]{1,0:T(8,128)(2,1)}, bf16[512,512]{1,0:T(8,128)(2,1)}) custom-call(s32[512,1]{1,0:T(8,128)} %sub.19.slot_ref, bf16[32,2,32,512]{3,2,1,0:T(8,128)(2,1)} %copy-done.1), custom_call_target="tpu_custom_call" | custom-call | tf_op jit(solution)/shard_map/unpack_slots/pallas_call | solution.py:73
  178.3 42.5 %reduce-scatter.7.cloned.1.call-done = bf16[128,1024]{1,0:T(8,128)(2,1)} async-done(((bf16[4096,1024]{1,0:T(8,128)(2,1)}), bf16[128,1024]{1,0:T(8,128)(2,1)}) %reduce-scatter.7.cloned.1.call-update) | async-done | bytes 262160
  220.7 1.1 copy.43
  221.9 0.8 copy.40
  222.8 0.8 copy.39
  223.6 46.7 %reduce-scatter.5.cloned.1.call-done = bf16[128,4096]{1,0:T(8,128)(2,1)} async-done(((bf16[512,4096]{1,0:T(8,128)(2,1)}), bf16[128,4096]{1,0:T(8,128)(2,1)}) %reduce-scatter.5.cloned.1.call-update) | async-done | bytes 1048592 | tf_op jit(solution)/shard_map/reduce_scatter | solution.py:191
  (24 shorter events, 2.1 us)
Async XLA Ops:
  7.2 16.5 %copy-start.2 = (s32[32,32]{1,0:T(8,128)S(1)}, s32[32,32]{1,0:T(8,128)}, u32[]{:S(2)}) copy-start(s32[32,32]{1,0:T(8,128)} %param.16) | copy-start | bytes 12292
  7.2 16.5 %copy-start.3 = (s32[32,32]{1,0:T(8,128)S(1)}, s32[32,32]{1,0:T(8,128)}, u32[]{:S(2)}) copy-start(s32[32,32]{1,0:T(8,128)} %param.17) | copy-start | bytes 12292
  7.2 76.3 %all-gather.2.cloned.1.call-start = ((), (), s32[]{:S(2)}) async-start(), calls=%async_computation.4 | async-start | bytes 8650752 | tf_op jit(solution)/shard_map/all_gather | solution.py:172
  16.2 77.4 %all-to-all-start = ((bf16[32,2,32,512]{3,2,1,0:T(8,128)(2,1)}), bf16[32,2,32,512]{3,2,1,0:T(8,128)(2,1)S(1)}, u32[]{:S(2)}, u32[]{:S(2)}) async-start(bf16[32,2,32,512]{3,2,1,0:T(8,128)(2,1)} %pack_slots.1), calls=%async_computation | async-start | bytes 4194304 | tf_op jit(solution)/shard_map/all_to_all | solution.py:176
  23.6 197.1 %reduce-scatter.7.cloned.1.call-start = ((), (), s32[]{:S(2)}) async-start(), calls=%async_computation.6 | async-start | bytes 8650752
  93.6 1.4 copy-start
  128.4 142.0 %reduce-scatter.5.cloned.1.call-start = ((), (), s32[]{:S(2)}) async-start(), calls=%async_computation.5 | async-start | bytes 5242880 | tf_op jit(solution)/shard_map/reduce_scatter | solution.py:191
  137.9 35.5 %all-to-all-start.1 = ((bf16[32,2,32,512]{3,2,1,0:T(8,128)(2,1)}), bf16[32,2,32,512]{3,2,1,0:T(8,128)(2,1)S(1)}, u32[]{:S(2)}, u32[]{:S(2)}) async-start(bf16[32,2,32,512]{3,2,1,0:T(8,128)(2,1)} %get-tuple-element.9), calls=%async_computation.1 | async-start | bytes 4194304 | tf_op jit(solution)/shard_map/all_to_all | solution.py:188
  173.4 1.3 copy-start.1
Sparse Core Ops, SparseCore 0:
  10.9 72.5 all-gather.1
  128.5 92.2 reduce-scatter.6
  223.9 46.4 reduce-scatter.4

commit v2 on v1

--- a/solution.py
+++ b/solution.py
@@ -87,7 +87,16 @@
 
 
 def attend_body(
-    wanted_ref, segment_ref, in_ref, key_ref, value_ref, out_ref, grad_kv_ref, key_sum, value_sum
+    wanted_ref,
+    segment_ref,
+    in_ref,
+    key_ref,
+    value_ref,
+    out_ref,
+    grad_key_ref,
+    grad_value_ref,
+    key_sum,
+    value_sum,
 ):
     block = pl.program_id(1)
     rows = BLOCK_PEERS * DEPTH
@@ -122,8 +131,8 @@
 
     @pl.when(block == pl.num_programs(1) - 1)
     def _():
-        grad_kv_ref[0] = key_sum[...].astype(jnp.bfloat16)
-        grad_kv_ref[1] = value_sum[...].astype(jnp.bfloat16)
+        grad_key_ref[...] = key_sum[...].astype(jnp.bfloat16)
+        grad_value_ref[...] = value_sum[...].astype(jnp.bfloat16)
 
 
 def attend(wanted, segment, arrived, kv):
@@ -144,15 +153,67 @@
         ],
         out_specs=[
             pl.BlockSpec((BLOCK_PEERS, 2, DEPTH, HD), lambda h, i: (i, 0, 0, h)),
-            pl.BlockSpec((2, memory_rows, HD), lambda h, i: (0, 0, h)),
+            pl.BlockSpec((memory_rows, HD), lambda h, i: (0, h)),
+            pl.BlockSpec((memory_rows, HD), lambda h, i: (0, h)),
         ],
         out_shape=[
             jax.ShapeDtypeStruct(arrived.shape, jnp.bfloat16),
-            jax.ShapeDtypeStruct((2, memory_rows, width), jnp.bfloat16),
+            jax.ShapeDtypeStruct((memory_rows, width), jnp.bfloat16),
+            jax.ShapeDtypeStruct((memory_rows, width), jnp.bfloat16),
         ],
         scratch_shapes=[pltpu.VMEM((memory_rows, HD), jnp.float32)] * 2,
         name="attend",
     )(wanted_rows, segment.reshape(1, memory_rows), arrived, kv, kv)
+
+
+def weight_body(memory_ref, grad_key_ref, grad_value_ref, out_ref):
+    width = grad_key_ref.shape[1]
+    columns = memory_ref[...]
+    out_ref[:, :width] = dot(columns, grad_key_ref[...], 0, 0).astype(jnp.bfloat16)
+    out_ref[:, width:] = dot(columns, grad_value_ref[...], 0, 0).astype(jnp.bfloat16)
+
+
+def weight_terms(memory, grad_keys, grad_values):
+    rows, model = memory.shape
+    width = grad_keys.shape[1]
+    block = 512
+    return pl.pallas_call(
+        weight_body,
+        grid=(model // block,),
+        in_specs=[
+            pl.BlockSpec((rows, block), lambda i: (0, i)),
+            pl.BlockSpec((rows, width), lambda i: (0, 0)),
+            pl.BlockSpec((rows, width), lambda i: (0, 0)),
+        ],
+        out_specs=pl.BlockSpec((block, 2 * width), lambda i: (i, 0)),
+        out_shape=jax.ShapeDtypeStruct((model, 2 * width), jnp.bfloat16),
+        name="weight_terms",
+    )(memory, grad_keys, grad_values)
+
+
+def memory_body(grad_key_ref, grad_value_ref, weight_ref, out_ref):
+    width = grad_key_ref.shape[1]
+    total = dot(grad_key_ref[...], weight_ref[:, :width], 1, 1)
+    total += dot(grad_value_ref[...], weight_ref[:, width:], 1, 1)
+    out_ref[...] = total.astype(jnp.bfloat16)
+
+
+def memory_terms(grad_keys, grad_values, weights):
+    rows, width = grad_keys.shape
+    model = weights.shape[0]
+    block = 512
+    return pl.pallas_call(
+        memory_body,
+        grid=(model // block,),
+        in_specs=[
+            pl.BlockSpec((rows, width), lambda i: (0, 0)),
+            pl.BlockSpec((rows, width), lambda i: (0, 0)),
+            pl.BlockSpec((block, 2 * width), lambda i: (i, 0)),
+        ],
+        out_specs=pl.BlockSpec((rows, block), lambda i: (0, i)),
+        out_shape=jax.ShapeDtypeStruct((rows, model), jnp.bfloat16),
+        name="memory_terms",
+    )(grad_keys, grad_values, weights)
 
 
 def per_device(
@@ -179,16 +240,23 @@
         jnp.any(owned, axis=1), jnp.sum(jnp.where(owned, example_slot, 0), axis=1), -1
     )
     kv = dot(memory, weights, 1, 0).astype(jnp.bfloat16)
-    answers, grad_kv = attend(wanted, memory_segment[0], arrived, kv)
-    grad_kv = jnp.concatenate((grad_kv[0], grad_kv[1]), axis=1)
-    weight_terms = dot(memory, grad_kv, 0, 0).astype(jnp.bfloat16)
+    answers, grad_keys, grad_values = attend(wanted, memory_segment[0], arrived, kv)
     weight_grads = lax.psum_scatter(
-        weight_terms, "dp", scatter_dimension=0, tiled=True
+        weight_terms(memory, grad_keys, grad_values), "dp", scatter_dimension=0, tiled=True
     ).astype(jnp.float32)
     returned = lax.all_to_all(answers, "dp", split_axis=0, concat_axis=0, tiled=True)
     context, grad_query = unpack_slots(slots, returned)
-    partial_sums = dot(grad_kv, weights, 1, 1).astype(jnp.bfloat16)
-    grad_memory = lax.psum_scatter(partial_sums, "fsdp", scatter_dimension=0, tiled=True)
+    terms = lax.all_to_all(
+        memory_terms(grad_keys, grad_values, weights),
+        "fsdp",
+        split_axis=0,
+        concat_axis=0,
+        tiled=True,
+    )
+    groups = lax.axis_size("fsdp")
+    grad_memory = jnp.sum(
+        terms.reshape(groups, terms.shape[0] // groups, terms.shape[1]).astype(jnp.float32), axis=0
+    ).astype(jnp.bfloat16)
     return (
         context,
         grad_query,

time: 279 us -> 220 us (0.79)
  waiting for transfers between devices: 176 us -> 120 us
  Pallas kernels: 18.9 us -> 40.2 us
  matrix products: 28.6 us -> 10.1 us
  local copies, waits for them, and re-layouts: 21.2 us -> 6.9 us
  starting transfers between devices: 13 us -> 17.9 us
  other arithmetic: 5.04 us -> 9.27 us
    reduce_scatter x1, waiting for transfers between devices: 46.7 us -> 0.01 us  [per_device(): lax.psum_scatter(weight_terms(memory, grad_keys, grad_values), 'dp', scat...]
    all_to_all x0 -> x1, waiting for transfers between devices: none -> 42.8 us  [per_device(): lax.all_to_all(memory_terms(grad_keys, grad_values, weights), 'fsdp', spl...]
    unnamed x4 -> x2, waiting for transfers between devices: 42.5 us -> 0.03 us
    pallas_call x0 -> x2, Pallas kernels: none -> 21.4 us  [the longest x1 10.9 us: memory_terms(): pl.pallas_call(memory_body, grid=(model // block,), in_specs=[pl.BlockSpe...]
    dot_general x3 -> x1, matrix products: 28.6 us -> 10.1 us  [dot(): lax.dot_general(left, right, (((left_dim,), (right_dim,)), ((), ())), pre...]
    unnamed x12 -> x8, local copies, waits for them, and re-layouts: 17.4 us -> 2.68 us
    all_to_all x1, waiting for transfers between devices: 28.9 us -> 19.1 us  [per_device(): lax.all_to_all(answers, 'dp', split_axis=0, concat_axis=0, tiled=True)]
    all_to_all x0 -> x1, starting transfers between devices: none -> 4.94 us  [per_device(): lax.all_to_all(memory_terms(grad_keys, grad_values, weights), 'fsdp', spl...]
  transfers between devices with their start and end apart: 5 -> 5, of which waited for: 4 -> 3; matrix products, arithmetic and copies ran while one was open for 10% -> 9% of each run, Pallas kernels for 3% -> 9%
where the time goes in v2:
time: 220 us; the launch traced here: 219 us
  waiting for transfers between devices  120 us (55%)
  Pallas kernels  40.2 us (18%)
  starting transfers between devices  17.9 us (8%)
  between operations  14.1 us (6%)
  matrix products  10.1 us (5%)
  other arithmetic  9.27 us (4%)
  local copies, waits for them, and re-layouts  6.9 us (3%)
    all_gather x1, waiting for transfers between devices, per_device(): weights = lax.all_gather(stacked, 'dp', axis=0, tiled=True)  58.2 us
    all_to_all x1, waiting for transfers between devices, per_device(): lax.all_to_all(memory_terms(grad_keys, grad_values, weights), 'fsdp', spl...  42.8 us
    all_to_all x1, waiting for transfers between devices, per_device(): lax.all_to_all(answers, 'dp', split_axis=0, concat_axis=0, tiled=True)  19.1 us
    pallas_call x1, Pallas kernels, attend(): pl.pallas_call(attend_body, grid=(heads, PEERS // BLOCK_PEERS), in_specs=...  11.1 us
    pallas_call x1, Pallas kernels, memory_terms(): pl.pallas_call(memory_body, grid=(model // block,), in_specs=[pl.BlockSpe...  10.9 us
    pallas_call x1, Pallas kernels, weight_terms(): pl.pallas_call(weight_body, grid=(model // block,), in_specs=[pl.BlockSpe...  10.5 us
    dot_general x1, matrix products, dot(): lax.dot_general(left, right, (((left_dim,), (right_dim,)), ((), ())), pre...  10.1 us
    all_to_all x1, starting transfers between devices, per_device(): lax.all_to_all(outgoing, 'dp', split_axis=0, concat_axis=0, tiled=True)  7.4 us
  transfers between devices with their start and end apart: 5, of which 3 were waited for; matrix products, arithmetic and copies ran while one was open for 9% of the time, Pallas kernels for 9%

profile of v2, /device:TPU:0, one launch (start us, length us, event | category | flops | bytes accessed | tf_op | source)
XLA Modules:
  0.0 218.7 jit_solution(8435242980352194221)
XLA Ops:
  7.2 1.7 pad_maximum_fusion
  9.0 0.7 dynamic-slice_bitcast_fusion
  9.7 0.8 select_reduce_fusion
  10.4 1.0 convert_reduce_fusion
  11.4 0.6 add_subtract_fusion.slot_ref
  12.0 4.1 %pack_slots.1 = bf16[32,2,32,512]{3,2,1,0:T(8,128)(2,1)} custom-call(s32[1,512]{1,0:T(1,128)} %add_subtract_fusion.slot_ref, bf16[512,512]{1,0:T(8,128)(2,1)} %query_ref.1, bf16[512,512]{1,0:T(8,128)(2,1)} %grad_ref.1), custom_call_target="tpu_custom_call" | custom-call | tf_op jit(solution)/shard_map/pack_slots/pallas_call | solution.py:46
  16.2 7.4 %all-to-all-start = ((bf16[32,2,32,512]{3,2,1,0:T(8,128)(2,1)}), bf16[32,2,32,512]{3,2,1,0:T(8,128)(2,1)S(1)}, u32[]{:S(2)}, u32[]{:S(2)}) async-start(bf16[32,2,32,512]{3,2,1,0:T(8,128)(2,1)} %pack_slots.1), calls=%async_computation | async-start | bytes 4194304 | tf_op jit(solution)/shard_map/all_to_all | solution.py:237
  24.0 1.3 reshape.72.wanted_ref
  25.3 58.2 %all-gather.2.cloned.1.call-done.weight_ref = bf16[4096,1024]{1,0:T(8,128)(2,1)} async-done(((bf16[128,1024]{1,0:T(8,128)(2,1)}), bf16[4096,1024]{1,0:T(8,128)(2,1)}) %all-gather.2.cloned.1.call-update) | async-done | bytes 8388624 | tf_op jit(solution)/shard_map/all_gather | solution.py:233
  83.5 10.1 %fusion.key_ref.value_ref = bf16[512,1024]{1,0:T(8,128)(2,1)} fusion(bf16[512,4096]{1,0:T(8,128)(2,1)} %memory_ref.1, bf16[4096,1024]{1,0:T(8,128)(2,1)} %all-gather.2.cloned.1.call-done.weight_ref), kind=kOutput, calls=%fused_computation.1 | convolution fusion | flops 4295491584 | bytes 13631488 | tf_op jit(solution)/shard_map/dot_general | solution.py:19
  93.7 1.3 copy-done
  95.0 11.1 %attend.1 = (bf16[32,2,32,512]{3,2,1,0:T(8,128)(2,1)}, bf16[512,512]{1,0:T(8,128)(2,1)}, bf16[512,512]{1,0:T(8,128)(2,1)}) custom-call(s32[1024,1]{1,0:T(8,128)} %reshape.72.wanted_ref, s32[1,512]{1,0:T(1,128)} %segment_ref.1, bf16[32,2,32,512]{3,2,1,0:T(8,128)(2,1)} %copy-done, bf16[512,1024]{1,0:T(8,128)(2,1)} %fusion.key_ref.value_ref, ...), custom_call_target="tpu_custom_call" | custom-call | tf_op jit(solution)/shard_map/attend/pallas_call | solution.py:144
  106.1 10.5 %weight_terms.1 = bf16[4096,1024]{1,0:T(8,128)(2,1)} custom-call(bf16[512,4096]{1,0:T(8,128)(2,1)} %memory_ref.1, bf16[512,512]{1,0:T(8,128)(2,1)} %get-tuple-element.13.grad_key_ref, bf16[512,512]{1,0:T(8,128)(2,1)} %get-tuple-element.14.grad_value_ref), custom_call_target="tpu_custom_call" | custom-call | tf_op jit(solution)/shard_map/weight_terms/pallas_call | solution.py:180
  116.6 5.5 %all-to-all-start.1 = ((bf16[32,2,32,512]{3,2,1,0:T(8,128)(2,1)}), bf16[32,2,32,512]{3,2,1,0:T(8,128)(2,1)S(1)}, u32[]{:S(2)}, u32[]{:S(2)}) async-start(bf16[32,2,32,512]{3,2,1,0:T(8,128)(2,1)} %get-tuple-element.10), calls=%async_computation.1 | async-start | bytes 4194304 | tf_op jit(solution)/shard_map/all_to_all | solution.py:247
  122.1 10.9 %memory_terms.1 = bf16[512,4096]{1,0:T(8,128)(2,1)} custom-call(bf16[512,512]{1,0:T(8,128)(2,1)} %get-tuple-element.13.grad_key_ref, bf16[512,512]{1,0:T(8,128)(2,1)} %get-tuple-element.14.grad_value_ref, bf16[4096,1024]{1,0:T(8,128)(2,1)} %all-gather.2.cloned.1.call-done.weight_ref), custom_call_target="tpu_custom_call" | custom-call | tf_op jit(solution)/shard_map/memory_terms/pallas_call | solution.py:205
  133.0 19.1 %all-to-all-done.1.in_ref = bf16[32,2,32,512]{3,2,1,0:T(8,128)(2,1)S(1)} async-done(((bf16[32,2,32,512]{3,2,1,0:T(8,128)(2,1)}), bf16[32,2,32,512]{3,2,1,0:T(8,128)(2,1)S(1)}, u32[]{:S(2)}, u32[]{:S(2)}) %all-to-all-start.1) | async-done | bytes 2097184 | tf_op jit(solution)/shard_map/all_to_all | solution.py:247
  152.1 1.3 copy-done.1
  153.4 4.9 %all-to-all-start.2 = ((bf16[4,128,4096]{2,1,0:T(8,128)(2,1)}), bf16[4,128,4096]{2,1,0:T(8,128)(2,1)}, u32[]{:S(2)}, u32[]{:S(2)}) async-start(bf16[4,128,4096]{2,1,0:T(8,128)(2,1)} %bitcast.12), calls=%async_computation.3 | async-start | bytes 8388608 | tf_op jit(solution)/shard_map/all_to_all | solution.py:249
  158.5 0.1 copy.24
  158.7 0.7 sub.19.slot_ref
  159.4 3.6 %unpack_slots.1 = (bf16[512,512]{1,0:T(8,128)(2,1)}, bf16[512,512]{1,0:T(8,128)(2,1)}) custom-call(s32[512,1]{1,0:T(8,128)} %sub.19.slot_ref, bf16[32,2,32,512]{3,2,1,0:T(8,128)(2,1)} %copy-done.1), custom_call_target="tpu_custom_call" | custom-call | tf_op jit(solution)/shard_map/unpack_slots/pallas_call | solution.py:73
  163.0 42.8 %all-to-all-done.2 = bf16[4,128,4096]{2,1,0:T(8,128)(2,1)} async-done(((bf16[4,128,4096]{2,1,0:T(8,128)(2,1)}), bf16[4,128,4096]{2,1,0:T(8,128)(2,1)}, u32[]{:S(2)}, u32[]{:S(2)}) %all-to-all-start.2) | async-done | bytes 4194336 | tf_op jit(solution)/shard_map/all_to_all | solution.py:249
  205.8 4.2 %reduce_sum.48 = bf16[128,4096]{1,0:T(8,128)(2,1)} reduce(bf16[4,128,4096]{2,1,0:T(8,128)(2,1)} %all-to-all-done.2, bf16[]{:T(256)} %constant.20.clone.1), dimensions={0}, to_apply=%region_5.6 | reduce | flops 1572864 | bytes 5242882 | tf_op jit(solution)/shard_map/reduce_sum | solution.py:257
  210.1 1.8 fusion.1
  (19 shorter events, 0.6 us)
Async XLA Ops:
  7.2 16.5 %copy-start.2 = (s32[32,32]{1,0:T(8,128)S(1)}, s32[32,32]{1,0:T(8,128)}, u32[]{:S(2)}) copy-start(s32[32,32]{1,0:T(8,128)} %param.16) | copy-start | bytes 12292
  7.2 16.5 %copy-start.3 = (s32[32,32]{1,0:T(8,128)S(1)}, s32[32,32]{1,0:T(8,128)}, u32[]{:S(2)}) copy-start(s32[32,32]{1,0:T(8,128)} %param.17) | copy-start | bytes 12292
  7.2 76.4 %all-gather.2.cloned.1.call-start = ((), (), s32[]{:S(2)}) async-start(), calls=%async_computation.4 | async-start | bytes 8650752 | tf_op jit(solution)/shard_map/all_gather | solution.py:233
  16.2 77.5 %all-to-all-start = ((bf16[32,2,32,512]{3,2,1,0:T(8,128)(2,1)}), bf16[32,2,32,512]{3,2,1,0:T(8,128)(2,1)S(1)}, u32[]{:S(2)}, u32[]{:S(2)}) async-start(bf16[32,2,32,512]{3,2,1,0:T(8,128)(2,1)} %pack_slots.1), calls=%async_computation | async-start | bytes 4194304 | tf_op jit(solution)/shard_map/all_to_all | solution.py:237
  23.6 186.5 %reduce-scatter.2.cloned.1.call-start = ((), (), s32[]{:S(2)}) async-start(), calls=%async_computation.5 | async-start | bytes 8650752 | tf_op jit(solution)/shard_map/reduce_scatter | solution.py:244
  93.7 1.3 copy-start
  116.6 35.5 %all-to-all-start.1 = ((bf16[32,2,32,512]{3,2,1,0:T(8,128)(2,1)}), bf16[32,2,32,512]{3,2,1,0:T(8,128)(2,1)S(1)}, u32[]{:S(2)}, u32[]{:S(2)}) async-start(bf16[32,2,32,512]{3,2,1,0:T(8,128)(2,1)} %get-tuple-element.10), calls=%async_computation.1 | async-start | bytes 4194304 | tf_op jit(solution)/shard_map/all_to_all | solution.py:247
  152.1 1.3 copy-start.1
  153.4 52.4 %all-to-all-start.2 = ((bf16[4,128,4096]{2,1,0:T(8,128)(2,1)}), bf16[4,128,4096]{2,1,0:T(8,128)(2,1)}, u32[]{:S(2)}, u32[]{:S(2)}) async-start(bf16[4,128,4096]{2,1,0:T(8,128)(2,1)} %bitcast.12), calls=%async_computation.3 | async-start | bytes 8388608 | tf_op jit(solution)/shard_map/all_to_all | solution.py:249
Sparse Core Ops, SparseCore 0:
  10.9 72.6 all-gather.1
  116.7 92.1 reduce-scatter.1

commit v3 on v2

--- a/solution.py
+++ b/solution.py
@@ -9,6 +9,7 @@
 PEERS = 32
 DEPTH = 32
 BLOCK_PEERS = 8
+RING = 4
 
 
 SCORE_SCALE = 0.0625
@@ -166,54 +167,154 @@
     )(wanted_rows, segment.reshape(1, memory_rows), arrived, kv, kv)
 
 
-def weight_body(memory_ref, grad_key_ref, grad_value_ref, out_ref):
+def peer_of(y, x, core):
+    return (y % RING) * 2 * RING + (x % RING) * 2 + core
+
+
+def shift(y_step, x_step, swap):
+    return [
+        (peer_of(y, x, core), peer_of(y + y_step, x + x_step, core ^ swap))
+        for y in range(RING)
+        for x in range(RING)
+        for core in range(2)
+    ]
+
+
+def relative_table(core):
+    index = lax.axis_index("dp")
+    steps = jnp.arange(RING * RING, dtype=jnp.int32)
+    return peer_of(index // (2 * RING) + steps // RING, index // 2 % RING + steps % RING, core)
+
+
+def away_body(table_ref, memory_ref, grad_key_ref, grad_value_ref, out_ref):
+    del table_ref
     width = grad_key_ref.shape[1]
     columns = memory_ref[...]
     out_ref[:, :width] = dot(columns, grad_key_ref[...], 0, 0).astype(jnp.bfloat16)
     out_ref[:, width:] = dot(columns, grad_value_ref[...], 0, 0).astype(jnp.bfloat16)
 
 
-def weight_terms(memory, grad_keys, grad_values):
+def away_terms(table, memory, grad_keys, grad_values):
     rows, model = memory.shape
     width = grad_keys.shape[1]
-    block = 512
-    return pl.pallas_call(
-        weight_body,
-        grid=(model // block,),
-        in_specs=[
-            pl.BlockSpec((rows, block), lambda i: (0, i)),
-            pl.BlockSpec((rows, width), lambda i: (0, 0)),
-            pl.BlockSpec((rows, width), lambda i: (0, 0)),
-        ],
-        out_specs=pl.BlockSpec((block, 2 * width), lambda i: (i, 0)),
-        out_shape=jax.ShapeDtypeStruct((model, 2 * width), jnp.bfloat16),
-        name="weight_terms",
-    )(memory, grad_keys, grad_values)
-
-
-def memory_body(grad_key_ref, grad_value_ref, weight_ref, out_ref):
+    block = model // PEERS
+    steps = RING * RING
+    return pl.pallas_call(
+        away_body,
+        grid_spec=pltpu.PrefetchScalarGridSpec(
+            num_scalar_prefetch=1,
+            grid=(steps,),
+            in_specs=[
+                pl.BlockSpec((rows, block), lambda i, table: (0, table[i])),
+                pl.BlockSpec((rows, width), lambda i, table: (0, 0)),
+                pl.BlockSpec((rows, width), lambda i, table: (0, 0)),
+            ],
+            out_specs=pl.BlockSpec((block, 2 * width), lambda i, table: (i, 0)),
+        ),
+        out_shape=jax.ShapeDtypeStruct((steps * block, 2 * width), jnp.bfloat16),
+        name="away_terms",
+    )(table, memory, grad_keys, grad_values)
+
+
+def home_body(table_ref, memory_ref, grad_key_ref, grad_value_ref, other_ref, *out_refs):
+    del table_ref
+    y_step = pl.program_id(0)
+    x_step = pl.program_id(1)
     width = grad_key_ref.shape[1]
+    half = other_ref.shape[0] // 2
+    columns = memory_ref[...]
+    for start, grad_ref in ((0, grad_key_ref), (width, grad_value_ref)):
+        total = dot(columns, grad_ref[...], 0, 0)
+        total += other_ref[:, start : start + width].astype(jnp.float32)
+        total = total.astype(jnp.bfloat16)
+        for step in range(RING):
+
+            @pl.when(y_step == step)
+            def _():
+                out_refs[step][x_step, :, start : start + width] = total[:half]
+
+            @pl.when(x_step == step)
+            def _():
+                out_refs[RING + step][y_step, :, start : start + width] = total[half:]
+
+
+def home_terms(table, memory, grad_keys, grad_values, other):
+    rows, model = memory.shape
+    width = grad_keys.shape[1]
+    block = model // PEERS
+    piece = (RING, block // 2, 2 * width)
+    return pl.pallas_call(
+        home_body,
+        grid_spec=pltpu.PrefetchScalarGridSpec(
+            num_scalar_prefetch=1,
+            grid=(RING, RING),
+            in_specs=[
+                pl.BlockSpec((rows, block), lambda i, j, table: (0, table[i * RING + j])),
+                pl.BlockSpec((rows, width), lambda i, j, table: (0, 0)),
+                pl.BlockSpec((rows, width), lambda i, j, table: (0, 0)),
+                pl.BlockSpec((block, 2 * width), lambda i, j, table: (i * RING + j, 0)),
+            ],
+            out_specs=[pl.BlockSpec(piece, lambda i, j, table: (0, 0, 0))] * (2 * RING),
+        ),
+        out_shape=[jax.ShapeDtypeStruct(piece, jnp.bfloat16)] * (2 * RING),
+        name="home_terms",
+    )(table, memory, grad_keys, grad_values, other)
+
+
+def sum_pieces(pieces):
+    total = pieces[0].astype(jnp.float32)
+    for piece in pieces[1:]:
+        total += piece.astype(jnp.float32)
+    return total
+
+
+def ring_exchange(pieces, along_y):
+    received = [pieces[0]]
+    for step in range(1, RING):
+        perm = shift(step, 0, 0) if along_y else shift(0, step, 0)
+        received.append(lax.ppermute(pieces[step], "dp", perm))
+    return received
+
+
+def first_sums(received):
+    return [
+        sum_pieces([piece[step] for piece in received]).astype(jnp.bfloat16)
+        for step in range(RING)
+    ]
+
+
+def memory_body(group_ref, grad_key_ref, grad_value_ref, weight_ref, *refs):
+    out_refs, total_ref = refs[:-1], refs[-1]
+    width = grad_key_ref.shape[1]
+    rows = out_refs[0].shape[0]
     total = dot(grad_key_ref[...], weight_ref[:, :width], 1, 1)
     total += dot(grad_value_ref[...], weight_ref[:, width:], 1, 1)
-    out_ref[...] = total.astype(jnp.bfloat16)
-
-
-def memory_terms(grad_keys, grad_values, weights):
+    total_ref[...] = total
+    for step, out_ref in enumerate(out_refs):
+        start = pl.multiple_of((group_ref[0] + step) % RING * rows, rows)
+        out_ref[...] = total_ref[pl.ds(start, rows), :].astype(jnp.bfloat16)
+
+
+def memory_terms(group, grad_keys, grad_values, weights):
     rows, width = grad_keys.shape
     model = weights.shape[0]
     block = 512
     return pl.pallas_call(
         memory_body,
-        grid=(model // block,),
-        in_specs=[
-            pl.BlockSpec((rows, width), lambda i: (0, 0)),
-            pl.BlockSpec((rows, width), lambda i: (0, 0)),
-            pl.BlockSpec((block, 2 * width), lambda i: (i, 0)),
-        ],
-        out_specs=pl.BlockSpec((rows, block), lambda i: (0, i)),
-        out_shape=jax.ShapeDtypeStruct((rows, model), jnp.bfloat16),
+        grid_spec=pltpu.PrefetchScalarGridSpec(
+            num_scalar_prefetch=1,
+            grid=(model // block,),
+            in_specs=[
+                pl.BlockSpec((rows, width), lambda i, group: (0, 0)),
+                pl.BlockSpec((rows, width), lambda i, group: (0, 0)),
+                pl.BlockSpec((block, 2 * width), lambda i, group: (i, 0)),
+            ],
+            out_specs=[pl.BlockSpec((rows // RING, block), lambda i, group: (0, i))] * RING,
+            scratch_shapes=[pltpu.VMEM((rows, block), jnp.float32)],
+        ),
+        out_shape=[jax.ShapeDtypeStruct((rows // RING, model), jnp.bfloat16)] * RING,
         name="memory_terms",
-    )(grad_keys, grad_values, weights)
+    )(group, grad_keys, grad_values, weights)
 
 
 def per_device(
@@ -241,22 +342,29 @@
     )
     kv = dot(memory, weights, 1, 0).astype(jnp.bfloat16)
     answers, grad_keys, grad_values = attend(wanted, memory_segment[0], arrived, kv)
-    weight_grads = lax.psum_scatter(
-        weight_terms(memory, grad_keys, grad_values), "dp", scatter_dimension=0, tiled=True
-    ).astype(jnp.float32)
     returned = lax.all_to_all(answers, "dp", split_axis=0, concat_axis=0, tiled=True)
+    core = my_index % 2
+    away = away_terms(relative_table(1 - core), memory, grad_keys, grad_values)
+    other = lax.ppermute(away, "dp", shift(0, 0, 1))
+    group = lax.axis_index("fsdp").astype(jnp.int32).reshape(1)
+    terms = memory_terms(group, grad_keys, grad_values, weights)
+    other, terms = lax.optimization_barrier((other, terms))
+    pieces = home_terms(relative_table(core), memory, grad_keys, grad_values, other)
+    arrived_terms = [terms[0]] + [
+        lax.ppermute(terms[step], "fsdp", [(i, (i + step) % RING) for i in range(RING)])
+        for step in range(1, RING)
+    ]
     context, grad_query = unpack_slots(slots, returned)
-    terms = lax.all_to_all(
-        memory_terms(grad_keys, grad_values, weights),
-        "fsdp",
-        split_axis=0,
-        concat_axis=0,
-        tiled=True,
-    )
-    groups = lax.axis_size("fsdp")
-    grad_memory = jnp.sum(
-        terms.reshape(groups, terms.shape[0] // groups, terms.shape[1]).astype(jnp.float32), axis=0
-    ).astype(jnp.bfloat16)
+    sums_y = first_sums(ring_exchange(pieces[:RING], True))
+    sums_x = first_sums(ring_exchange(pieces[RING:], False))
+    weight_grads = jnp.concatenate(
+        [
+            sum_pieces(ring_exchange(sums_y, False)),
+            sum_pieces(ring_exchange(sums_x, True)),
+        ],
+        axis=0,
+    )
+    grad_memory = sum_pieces(arrived_terms).astype(jnp.bfloat16)
     return (
         context,
         grad_query,

time: 220 us -> 242 us (1.10)
  waiting for transfers between devices: 120 us -> 93.8 us
  starting transfers between devices: 17.9 us -> 39.8 us
  Pallas kernels: 40.2 us -> 59.8 us
  other arithmetic: 9.27 us -> 16 us
    all_to_all x1 -> x0, waiting for transfers between devices: 42.8 us -> none  [per_device(): lax.all_to_all(memory_terms(grad_keys, grad_values, weights), 'fsdp', spl...]
    ppermute x0 -> x16, waiting for transfers between devices: none -> 36.4 us  [the longest x12 22.3 us: ring_exchange(): received.append(lax.ppermute(pieces[step], 'dp', perm))]
    ppermute x0 -> x16, starting transfers between devices: none -> 26.8 us  [the longest x12 20.7 us: ring_exchange(): received.append(lax.ppermute(pieces[step], 'dp', perm))]
    pallas_call x2 -> x3, Pallas kernels: 21.4 us -> 40.9 us  [the longest x1 17.1 us: home_terms(): pl.pallas_call(home_body, grid_spec=pltpu.PrefetchScalarGridSpec(num_scal...]
    all_to_all x1, waiting for transfers between devices: 19.1 us -> 0.01 us  [per_device(): lax.all_to_all(answers, 'dp', split_axis=0, concat_axis=0, tiled=True)]
    add x0 -> x5, other arithmetic: none -> 6.07 us  [the longest x4 5.48 us: sum_pieces(): total += piece.astype(jnp.float32)]
    all_to_all x1 -> x0, starting transfers between devices: 4.94 us -> none  [per_device(): lax.all_to_all(memory_terms(grad_keys, grad_values, weights), 'fsdp', spl...]
    reduce_sum x1 -> x0, other arithmetic: 4.24 us -> none  [per_device(): jnp.sum(terms.reshape(groups, terms.shape[0] // groups, terms.shape[1]).a...]
  transfers between devices with their start and end apart: 5 -> 19, of which waited for: 3 -> 7; matrix products, arithmetic and copies ran while one was open for 9% -> 10% of each run, Pallas kernels for 9% -> 15%
where the time goes in v3:
time: 242 us; the launch traced here: 240 us
  waiting for transfers between devices  93.8 us (39%)
  Pallas kernels  59.8 us (25%)
  starting transfers between devices  39.8 us (16%)
  other arithmetic  16 us (7%)
  between operations  14.2 us (6%)
  matrix products  10.1 us (4%)
  local copies, waits for them, and re-layouts  6.47 us (3%)
    all_gather x1, waiting for transfers between devices, per_device(): weights = lax.all_gather(stacked, 'dp', axis=0, tiled=True)  57.4 us
    ppermute x12, waiting for transfers between devices, ring_exchange(): received.append(lax.ppermute(pieces[step], 'dp', perm))  22.3 us
    ppermute x12, starting transfers between devices, ring_exchange(): received.append(lax.ppermute(pieces[step], 'dp', perm))  20.7 us
    pallas_call x1, Pallas kernels, home_terms(): pl.pallas_call(home_body, grid_spec=pltpu.PrefetchScalarGridSpec(num_scal...  17.1 us
    ppermute x3, waiting for transfers between devices, per_device(): lax.ppermute(terms[step], 'fsdp', [(i, (i + step) % RING) for i in range(...  14 us
    pallas_call x1, Pallas kernels, away_terms(): pl.pallas_call(away_body, grid_spec=pltpu.PrefetchScalarGridSpec(num_scal...  13.1 us
    pallas_call x1, Pallas kernels, attend(): pl.pallas_call(attend_body, grid=(heads, PEERS // BLOCK_PEERS), in_specs=...  11.1 us
    pallas_call x1, Pallas kernels, memory_terms(): pl.pallas_call(memory_body, grid_spec=pltpu.PrefetchScalarGridSpec(num_sc...  10.7 us
  transfers between devices with their start and end apart: 19, of which 7 were waited for; matrix products, arithmetic and copies ran while one was open for 10% of the time, Pallas kernels for 15%

profile of v3, /device:TPU:0, one launch (start us, length us, event | category | flops | bytes accessed | tf_op | source)
XLA Modules:
  0.0 240.2 jit_solution(17699949844747594728)
XLA Ops:
  12.0 4.2 %pack_slots.1 = bf16[32,2,32,512]{3,2,1,0:T(8,128)(2,1)} custom-call(s32[1,512]{1,0:T(1,128)} %add_subtract_fusion.slot_ref, bf16[512,512]{1,0:T(8,128)(2,1)} %query_ref.1, bf16[512,512]{1,0:T(8,128)(2,1)} %grad_ref.1), custom_call_target="tpu_custom_call" | custom-call | tf_op jit(solution)/shard_map/pack_slots/pallas_call | solution.py:47
  16.2 7.5 %all-to-all-start = ((bf16[32,2,32,512]{3,2,1,0:T(8,128)(2,1)}), bf16[32,2,32,512]{3,2,1,0:T(8,128)(2,1)S(1)}, u32[]{:S(2)}, u32[]{:S(2)}) async-start(bf16[32,2,32,512]{3,2,1,0:T(8,128)(2,1)} %pack_slots.1), calls=%async_computation | async-start | bytes 4194304 | tf_op jit(solution)/shard_map/all_to_all | solution.py:338
  26.1 57.4 %all-gather.2.cloned.1.call-done.weight_ref = bf16[4096,1024]{1,0:T(8,128)(2,1)} async-done(((bf16[128,1024]{1,0:T(8,128)(2,1)}), bf16[4096,1024]{1,0:T(8,128)(2,1)}) %all-gather.2.cloned.1.call-update) | async-done | bytes 8388624 | tf_op jit(solution)/shard_map/all_gather | solution.py:334
  83.5 10.1 %fusion.key_ref.value_ref = bf16[512,1024]{1,0:T(8,128)(2,1)} fusion(bf16[512,4096]{1,0:T(8,128)(2,1)} %memory_ref.3, bf16[4096,1024]{1,0:T(8,128)(2,1)} %all-gather.2.cloned.1.call-done.weight_ref), kind=kOutput, calls=%fused_computation.2 | convolution fusion | flops 4295491584 | bytes 13631488 | tf_op jit(solution)/shard_map/dot_general | solution.py:20
  94.9 11.1 %attend.1 = (bf16[32,2,32,512]{3,2,1,0:T(8,128)(2,1)}, bf16[512,512]{1,0:T(8,128)(2,1)}, bf16[512,512]{1,0:T(8,128)(2,1)}) custom-call(s32[1024,1]{1,0:T(8,128)} %reshape.138.wanted_ref, s32[1,512]{1,0:T(1,128)} %segment_ref.1, bf16[32,2,32,512]{3,2,1,0:T(8,128)(2,1)} %copy-done.1, bf16[512,1024]{1,0:T(8,128)(2,1)} %fusion.key_ref.value_ref, ...), custom_call_target="tpu_custom_call" | custom-call | tf_op jit(solution)/shard_map/attend/pallas_call | solution.py:145
  106.0 13.1 %away_terms.1 = bf16[2048,1024]{1,0:T(8,128)(2,1)} custom-call(s32[16]{0:T(128)} %get-tuple-element.59.table_ref, bf16[512,4096]{1,0:T(8,128)(2,1)} %memory_ref.3, bf16[512,512]{1,0:T(8,128)(2,1)} %get-tuple-element.30.grad_key_ref, bf16[512,512]{1,0:T(8,128)(2,1)} %get-tuple-element.31.grad_value_ref), custom_call_target="tpu_custom_call" | custom-call | tf_op jit(solution)/shard_map/away_terms/pallas_call | solution.py:202
  119.4 5.5 %all-to-all-start.1 = ((bf16[32,2,32,512]{3,2,1,0:T(8,128)(2,1)}), bf16[32,2,32,512]{3,2,1,0:T(8,128)(2,1)S(1)}, u32[]{:S(2)}, u32[]{:S(2)}) async-start(bf16[32,2,32,512]{3,2,1,0:T(8,128)(2,1)} %get-tuple-element.27), calls=%async_computation.1 | async-start | bytes 4194304 | tf_op jit(solution)/shard_map/all_to_all | solution.py:345
  124.9 10.7 %memory_terms.1 = (bf16[128,4096]{1,0:T(8,128)(2,1)}, bf16[128,4096]{1,0:T(8,128)(2,1)}, bf16[128,4096]{1,0:T(8,128)(2,1)}, bf16[128,4096]{1,0:T(8,128)(2,1)}) custom-call(s32[1]{0:T(128)} %bitcast.7.group_ref, bf16[512,512]{1,0:T(8,128)(2,1)} %get-tuple-element.30.grad_key_ref, bf16[512,512]{1,0:T(8,128)(2,1)} %get-tuple-element.31.grad_value_ref, ...), custom_call_target="tpu_custom_call" | custom-call | tf_op jit(solution)/shard_map/memory_terms/pallas_call | solution.py:302
  135.6 17.1 %home_terms.1 = (bf16[4,64,1024]{2,1,0:T(8,128)(2,1)}, bf16[4,64,1024]{2,1,0:T(8,128)(2,1)}, bf16[4,64,1024]{2,1,0:T(8,128)(2,1)}, bf16[4,64,1024]{2,1,0:T(8,128...) custom-call(s32[16]{0:T(128)} %get-tuple-element.60.table_ref, ...), custom_call_target="tpu_custom_call" | custom-call | tf_op jit(solution)/shard_map/home_terms/pallas_call | solution.py:246
  152.7 1.8 collective-permute-start.1
  154.5 2.7 %collective-permute-start.2 = (bf16[4,64,1024]{2,1,0:T(8,128)(2,1)}, bf16[4,64,1024]{2,1,0:T(8,128)(2,1)S(1)}, u32[]{:S(2)}, u32[]{:S(2)}) collective-permute-start(bf16[4,64,1024]{2,1,0:T(8,128)(2,1)} %get-tuple-element.39), channel_id=1, source_target_pairs={{0,64},{4,68},{8,72},{12,76},{16,80},{20,84},{24,88},{28,92},{32,9... | collective-permute-start | bytes 1572872 | tf_op jit(solution)/shard_map/ppermute | solution.py:275
  160.1 2.7 %collective-permute-start.8 = (bf16[4,64,1024]{2,1,0:T(8,128)(2,1)}, bf16[4,64,1024]{2,1,0:T(8,128)(2,1)S(1)}, u32[]{:S(2)}, u32[]{:S(2)}) collective-permute-start(bf16[4,64,1024]{2,1,0:T(8,128)(2,1)} %get-tuple-element.43), channel_id=1, source_target_pairs={{0,16},{4,20},{8,24},{12,28},{16,0},{20,4},{24,8},{28,12},{32,48},... | collective-permute-start | bytes 1572872 | tf_op jit(solution)/shard_map/ppermute | solution.py:275
  162.8 5.4 %collective-permute-done.1 = bf16[4,64,1024]{2,1,0:T(8,128)(2,1)S(1)} collective-permute-done((bf16[4,64,1024]{2,1,0:T(8,128)(2,1)}, bf16[4,64,1024]{2,1,0:T(8,128)(2,1)S(1)}, u32[]{:S(2)}, u32[]{:S(2)}) %collective-permute-start.1) | collective-permute-done | bytes 524320 | tf_op jit(solution)/shard_map/ppermute | solution.py:275
  168.2 2.9 %collective-permute-start.9 = (bf16[4,64,1024]{2,1,0:T(8,128)(2,1)}, bf16[4,64,1024]{2,1,0:T(8,128)(2,1)S(1)}, u32[]{:S(2)}, u32[]{:S(2)}) collective-permute-start(bf16[4,64,1024]{2,1,0:T(8,128)(2,1)} %get-tuple-element.44), channel_id=1, source_target_pairs={{0,24},{4,28},{8,0},{12,4},{16,8},{20,12},{24,16},{28,20},{32,56},... | collective-permute-start | bytes 1572872 | tf_op jit(solution)/shard_map/ppermute | solution.py:275
  171.1 9.5 %collective-permute-done.2 = bf16[4,64,1024]{2,1,0:T(8,128)(2,1)S(1)} collective-permute-done((bf16[4,64,1024]{2,1,0:T(8,128)(2,1)}, bf16[4,64,1024]{2,1,0:T(8,128)(2,1)S(1)}, u32[]{:S(2)}, u32[]{:S(2)}) %collective-permute-start.2) | collective-permute-done | bytes 524320 | tf_op jit(solution)/shard_map/ppermute | solution.py:275
  182.2 2.9 %collective-permute-start.14 = (bf16[128,4096]{1,0:T(8,128)(2,1)}, bf16[128,4096]{1,0:T(8,128)(2,1)}, u32[]{:S(2)}, u32[]{:S(2)}) collective-permute-start(bf16[128,4096]{1,0:T(8,128)(2,1)} %get-tuple-element.47), channel_id=1, source_target_pairs={{0,2},{1,3},{2,0},{3,1},{4,6},{5,7},{6,4},{7,5},{8,10},{9,11},{10,... | collective-permute-start | bytes 3145736 | tf_op jit(solution)/shard_map/ppermute | solution.py:354
  185.0 1.9 fusion.7
  192.5 2.0 collective-permute-done.4
  201.0 3.6 %unpack_slots.1 = (bf16[512,512]{1,0:T(8,128)(2,1)}, bf16[512,512]{1,0:T(8,128)(2,1)}) custom-call(s32[512,1]{1,0:T(8,128)} %sub.36.slot_ref, bf16[32,2,32,512]{3,2,1,0:T(8,128)(2,1)} %copy-done), custom_call_target="tpu_custom_call" | custom-call | tf_op jit(solution)/shard_map/unpack_slots/pallas_call | solution.py:74
  204.6 2.7 %collective-permute-start.12 = (bf16[64,1024]{1,0:T(8,128)(2,1)}, bf16[64,1024]{1,0:T(8,128)(2,1)S(1)}, u32[]{:S(2)}, u32[]{:S(2)}) collective-permute-start(bf16[64,1024]{1,0:T(8,128)(2,1)} %get-tuple-element.52), channel_id=1, source_target_pairs={{0,96},{4,100},{8,104},{12,108},{16,112},{20,116},{24,120},{28,124... | collective-permute-start | bytes 393224 | tf_op jit(solution)/shard_map/ppermute | solution.py:275
  208.6 2.9 %collective-permute-done.12 = bf16[64,1024]{1,0:T(8,128)(2,1)S(1)} collective-permute-done((bf16[64,1024]{1,0:T(8,128)(2,1)}, bf16[64,1024]{1,0:T(8,128)(2,1)S(1)}, u32[]{:S(2)}, u32[]{:S(2)}) %collective-permute-start.12) | collective-permute-done | bytes 131104 | tf_op jit(solution)/shard_map/ppermute | solution.py:275
  211.6 2.4 %collective-permute-done.11 = bf16[64,1024]{1,0:T(8,128)(2,1)S(1)} collective-permute-done((bf16[64,1024]{1,0:T(8,128)(2,1)}, bf16[64,1024]{1,0:T(8,128)(2,1)S(1)}, u32[]{:S(2)}, u32[]{:S(2)}) %collective-permute-start.11) | collective-permute-done | bytes 131104 | tf_op jit(solution)/shard_map/ppermute | solution.py:275
  216.1 14.0 %collective-permute-done.14 = bf16[128,4096]{1,0:T(8,128)(2,1)} collective-permute-done((bf16[128,4096]{1,0:T(8,128)(2,1)}, bf16[128,4096]{1,0:T(8,128)(2,1)}, u32[]{:S(2)}, u32[]{:S(2)}) %collective-permute-start.14) | collective-permute-done | bytes 1048608 | tf_op jit(solution)/shard_map/ppermute | solution.py:354
  230.2 3.2 %add_convert_fusion = bf16[128,4096]{1,0:T(8,128)(2,1)} fusion(bf16[128,4096]{1,0:T(8,128)(2,1)} %collective-permute-done.15, bf16[128,4096]{1,0:T(8,128)(2,1)} %collective-permute-done.14, bf16[128,4096]{1,0:T(8,128)(2,1)S(1)} %collective-permute-done.13, bf16[128,4096]{1,0:T(8,128)(2,1)S(1)} %copy-done.2), kind=kLoop, calls=%fused_computation | loop fusion | flops 4194304 | bytes 5242880 | tf_op jit(solution)/shard_map/convert_element_type | solution.py:367
  (72 shorter events, 28.6 us)
Async XLA Ops:
  7.2 76.3 %all-gather.2.cloned.1.call-start = ((), (), s32[]{:S(2)}) async-start(), calls=%async_computation.2 | async-start | bytes 8650752 | tf_op jit(solution)/shard_map/all_gather | solution.py:334
  16.2 77.4 %all-to-all-start = ((bf16[32,2,32,512]{3,2,1,0:T(8,128)(2,1)}), bf16[32,2,32,512]{3,2,1,0:T(8,128)(2,1)S(1)}, u32[]{:S(2)}, u32[]{:S(2)}) async-start(bf16[32,2,32,512]{3,2,1,0:T(8,128)(2,1)} %pack_slots.1), calls=%async_computation | async-start | bytes 4194304 | tf_op jit(solution)/shard_map/all_to_all | solution.py:338
  119.2 16.4 %collective-permute-start = (bf16[2048,1024]{1,0:T(8,128)(2,1)}, bf16[2048,1024]{1,0:T(8,128)(2,1)}, u32[]{:S(2)}, u32[]{:S(2)}) collective-permute-start(bf16[2048,1024]{1,0:T(8,128)(2,1)} %away_terms.1), channel_id=1, source_target_pairs={{0,4},{4,0},{8,12},{12,8},{16,20},{20,16},{24,28},{28,24},{32,36},... | collective-permute-start | bytes 12582920 | tf_op jit(solution)/shard_map/ppermute | solution.py:348
  119.4 80.2 %all-to-all-start.1 = ((bf16[32,2,32,512]{3,2,1,0:T(8,128)(2,1)}), bf16[32,2,32,512]{3,2,1,0:T(8,128)(2,1)S(1)}, u32[]{:S(2)}, u32[]{:S(2)}) async-start(bf16[32,2,32,512]{3,2,1,0:T(8,128)(2,1)} %get-tuple-element.27), calls=%async_computation.1 | async-start | bytes 4194304 | tf_op jit(solution)/shard_map/all_to_all | solution.py:345
  152.7 38.9 %copy-start.3 = (bf16[4,64,1024]{2,1,0:T(8,128)(2,1)S(1)}, bf16[4,64,1024]{2,1,0:T(8,128)(2,1)}, u32[]{:S(2)}) copy-start(bf16[4,64,1024]{2,1,0:T(8,128)(2,1)} %get-tuple-element.41) | copy-start | bytes 1572868
  152.7 15.5 %collective-permute-start.1 = (bf16[4,64,1024]{2,1,0:T(8,128)(2,1)}, bf16[4,64,1024]{2,1,0:T(8,128)(2,1)S(1)}, u32[]{:S(2)}, u32[]{:S(2)}) collective-permute-start(bf16[4,64,1024]{2,1,0:T(8,128)(2,1)} %get-tuple-element.38), channel_id=1, source_target_pairs={{0,32},{4,36},{8,40},{12,44},{16,48},{20,52},{24,56},{28,60},{32,6... | collective-permute-start | bytes 1572872 | tf_op jit(solution)/shard_map/ppermute | solution.py:275
  154.5 26.1 %collective-permute-start.2 = (bf16[4,64,1024]{2,1,0:T(8,128)(2,1)}, bf16[4,64,1024]{2,1,0:T(8,128)(2,1)S(1)}, u32[]{:S(2)}, u32[]{:S(2)}) collective-permute-start(bf16[4,64,1024]{2,1,0:T(8,128)(2,1)} %get-tuple-element.39), channel_id=1, source_target_pairs={{0,64},{4,68},{8,72},{12,76},{16,80},{20,84},{24,88},{28,92},{32,9... | collective-permute-start | bytes 1572872 | tf_op jit(solution)/shard_map/ppermute | solution.py:275
  157.2 25.0 %collective-permute-start.3 = (bf16[4,64,1024]{2,1,0:T(8,128)(2,1)}, bf16[4,64,1024]{2,1,0:T(8,128)(2,1)S(1)}, u32[]{:S(2)}, u32[]{:S(2)}) collective-permute-start(bf16[4,64,1024]{2,1,0:T(8,128)(2,1)} %get-tuple-element.40), channel_id=1, source_target_pairs={{0,96},{4,100},{8,104},{12,108},{16,112},{20,116},{24,120},{28,124... | collective-permute-start | bytes 1572872 | tf_op jit(solution)/shard_map/ppermute | solution.py:275
  158.6 28.3 %collective-permute-start.7 = (bf16[4,64,1024]{2,1,0:T(8,128)(2,1)}, bf16[4,64,1024]{2,1,0:T(8,128)(2,1)S(1)}, u32[]{:S(2)}, u32[]{:S(2)}) collective-permute-start(bf16[4,64,1024]{2,1,0:T(8,128)(2,1)} %get-tuple-element.42), channel_id=1, source_target_pairs={{0,8},{4,12},{8,16},{12,20},{16,24},{20,28},{24,0},{28,4},{32,40},... | collective-permute-start | bytes 1572872 | tf_op jit(solution)/shard_map/ppermute | solution.py:275
  160.1 28.3 %collective-permute-start.8 = (bf16[4,64,1024]{2,1,0:T(8,128)(2,1)}, bf16[4,64,1024]{2,1,0:T(8,128)(2,1)S(1)}, u32[]{:S(2)}, u32[]{:S(2)}) collective-permute-start(bf16[4,64,1024]{2,1,0:T(8,128)(2,1)} %get-tuple-element.43), channel_id=1, source_target_pairs={{0,16},{4,20},{8,24},{12,28},{16,0},{20,4},{24,8},{28,12},{32,48},... | collective-permute-start | bytes 1572872 | tf_op jit(solution)/shard_map/ppermute | solution.py:275
  168.2 28.1 %copy-start.6 = (bf16[4,64,1024]{2,1,0:T(8,128)(2,1)}, bf16[4,64,1024]{2,1,0:T(8,128)(2,1)S(1)}, u32[]{:S(2)}) copy-start(bf16[4,64,1024]{2,1,0:T(8,128)(2,1)S(1)} %collective-permute-done.1) | copy-start | bytes 1572868
  168.2 21.6 %collective-permute-start.9 = (bf16[4,64,1024]{2,1,0:T(8,128)(2,1)}, bf16[4,64,1024]{2,1,0:T(8,128)(2,1)S(1)}, u32[]{:S(2)}, u32[]{:S(2)}) collective-permute-start(bf16[4,64,1024]{2,1,0:T(8,128)(2,1)} %get-tuple-element.44), channel_id=1, source_target_pairs={{0,24},{4,28},{8,0},{12,4},{16,8},{20,12},{24,16},{28,20},{32,56},... | collective-permute-start | bytes 1572872 | tf_op jit(solution)/shard_map/ppermute | solution.py:275
  180.6 15.7 %copy-start.7 = (bf16[4,64,1024]{2,1,0:T(8,128)(2,1)}, bf16[4,64,1024]{2,1,0:T(8,128)(2,1)S(1)}, u32[]{:S(2)}) copy-start(bf16[4,64,1024]{2,1,0:T(8,128)(2,1)S(1)} %collective-permute-done.2) | copy-start | bytes 1572868
  180.6 35.5 %collective-permute-start.13 = (bf16[128,4096]{1,0:T(8,128)(2,1)}, bf16[128,4096]{1,0:T(8,128)(2,1)S(1)}, u32[]{:S(2)}, u32[]{:S(2)}) collective-permute-start(bf16[128,4096]{1,0:T(8,128)(2,1)} %get-tuple-element.46), channel_id=1, source_target_pairs={{0,1},{1,2},{2,3},{3,0},{4,5},{5,6},{6,7},{7,4},{8,9},{9,10},{10,1... | collective-permute-start | bytes 3145736 | tf_op jit(solution)/shard_map/ppermute | solution.py:354
  182.2 14.2 %copy-start.8 = (bf16[4,64,1024]{2,1,0:T(8,128)(2,1)}, bf16[4,64,1024]{2,1,0:T(8,128)(2,1)S(1)}, u32[]{:S(2)}) copy-start(bf16[4,64,1024]{2,1,0:T(8,128)(2,1)S(1)} %collective-permute-done.3) | copy-start | bytes 1572868
  182.2 48.0 %collective-permute-start.14 = (bf16[128,4096]{1,0:T(8,128)(2,1)}, bf16[128,4096]{1,0:T(8,128)(2,1)}, u32[]{:S(2)}, u32[]{:S(2)}) collective-permute-start(bf16[128,4096]{1,0:T(8,128)(2,1)} %get-tuple-element.47), channel_id=1, source_target_pairs={{0,2},{1,3},{2,0},{3,1},{4,6},{5,7},{6,4},{7,5},{8,10},{9,11},{10,... | collective-permute-start | bytes 3145736 | tf_op jit(solution)/shard_map/ppermute | solution.py:354
  187.0 43.2 %collective-permute-start.15 = (bf16[128,4096]{1,0:T(8,128)(2,1)}, bf16[128,4096]{1,0:T(8,128)(2,1)}, u32[]{:S(2)}, u32[]{:S(2)}) collective-permute-start(bf16[128,4096]{1,0:T(8,128)(2,1)} %get-tuple-element.48), channel_id=1, source_target_pairs={{0,3},{1,0},{2,1},{3,2},{4,7},{5,4},{6,5},{7,6},{8,11},{9,8},{10,9... | collective-permute-start | bytes 3145736 | tf_op jit(solution)/shard_map/ppermute | solution.py:354
  188.3 6.2 %collective-permute-start.4 = (bf16[64,1024]{1,0:T(8,128)(2,1)S(1)}, bf16[64,1024]{1,0:T(8,128)(2,1)S(1)}, u32[]{:S(2)}, u32[]{:S(2)}) collective-permute-start(bf16[64,1024]{1,0:T(8,128)(2,1)S(1)} %get-tuple-element.54), channel_id=1, source_target_pairs={{0,8},{4,12},{8,16},{12,20},{16,24},{20,28},{24,0},{28,4},{32,40},... | collective-permute-start | bytes 393224 | tf_op jit(solution)/shard_map/ppermute | solution.py:275
  189.8 6.5 %collective-permute-start.6 = (bf16[64,1024]{1,0:T(8,128)(2,1)S(1)}, bf16[64,1024]{1,0:T(8,128)(2,1)S(1)}, u32[]{:S(2)}, u32[]{:S(2)}) collective-permute-start(bf16[64,1024]{1,0:T(8,128)(2,1)S(1)} %get-tuple-element.55), channel_id=1, source_target_pairs={{0,24},{4,28},{8,0},{12,4},{16,8},{20,12},{24,16},{28,20},{32,56},... | collective-permute-start | bytes 393224 | tf_op jit(solution)/shard_map/ppermute | solution.py:275
  194.5 10.1 %collective-permute-start.5 = (bf16[64,1024]{1,0:T(8,128)(2,1)}, bf16[64,1024]{1,0:T(8,128)(2,1)}, u32[]{:S(2)}, u32[]{:S(2)}) collective-permute-start(bf16[64,1024]{1,0:T(8,128)(2,1)} %get-tuple-element.56), channel_id=1, source_target_pairs={{0,16},{4,20},{8,24},{12,28},{16,0},{20,4},{24,8},{28,12},{32,48},... | collective-permute-start | bytes 393224 | tf_op jit(solution)/shard_map/ppermute | solution.py:275
  196.3 11.0 %collective-permute-start.10 = (bf16[64,1024]{1,0:T(8,128)(2,1)}, bf16[64,1024]{1,0:T(8,128)(2,1)}, u32[]{:S(2)}, u32[]{:S(2)}) collective-permute-start(bf16[64,1024]{1,0:T(8,128)(2,1)} %get-tuple-element.51), channel_id=1, source_target_pairs={{0,32},{4,36},{8,40},{12,44},{16,48},{20,52},{24,56},{28,60},{32,6... | collective-permute-start | bytes 393224 | tf_op jit(solution)/shard_map/ppermute | solution.py:275
  204.6 25.6 %copy-start.2 = (bf16[128,4096]{1,0:T(8,128)(2,1)S(1)}, bf16[128,4096]{1,0:T(8,128)(2,1)}, u32[]{:S(2)}) copy-start(bf16[128,4096]{1,0:T(8,128)(2,1)} %get-tuple-element.45) | copy-start | bytes 3145732
  204.6 6.9 %collective-permute-start.12 = (bf16[64,1024]{1,0:T(8,128)(2,1)}, bf16[64,1024]{1,0:T(8,128)(2,1)S(1)}, u32[]{:S(2)}, u32[]{:S(2)}) collective-permute-start(bf16[64,1024]{1,0:T(8,128)(2,1)} %get-tuple-element.52), channel_id=1, source_target_pairs={{0,96},{4,100},{8,104},{12,108},{16,112},{20,116},{24,120},{28,124... | collective-permute-start | bytes 393224 | tf_op jit(solution)/shard_map/ppermute | solution.py:275
  207.3 6.7 %collective-permute-start.11 = (bf16[64,1024]{1,0:T(8,128)(2,1)}, bf16[64,1024]{1,0:T(8,128)(2,1)S(1)}, u32[]{:S(2)}, u32[]{:S(2)}) collective-permute-start(bf16[64,1024]{1,0:T(8,128)(2,1)} %get-tuple-element.53), channel_id=1, source_target_pairs={{0,64},{4,68},{8,72},{12,76},{16,80},{20,84},{24,88},{28,92},{32,9... | collective-permute-start | bytes 393224 | tf_op jit(solution)/shard_map/ppermute | solution.py:275
  (9 other events, 50.2 us)
Sparse Core Ops, SparseCore 0:
  10.8 72.5 all-gather.1

commit v4 on v3

--- a/solution.py
+++ b/solution.py
@@ -186,10 +186,22 @@
     return peer_of(index // (2 * RING) + steps // RING, index // 2 % RING + steps % RING, core)
 
 
-def away_body(table_ref, memory_ref, grad_key_ref, grad_value_ref, out_ref):
+def joined_columns(refs):
+    return jnp.concatenate([ref[...] for ref in refs], axis=1)
+
+
+def column_specs(rows, block):
+    return [
+        pl.BlockSpec((rows, block), lambda i, table, j=j: (0, table[i * RING + j]))
+        for j in range(RING)
+    ]
+
+
+def away_body(table_ref, *refs):
     del table_ref
+    grad_key_ref, grad_value_ref, out_ref = refs[RING:]
     width = grad_key_ref.shape[1]
-    columns = memory_ref[...]
+    columns = joined_columns(refs[:RING])
     out_ref[:, :width] = dot(columns, grad_key_ref[...], 0, 0).astype(jnp.bfloat16)
     out_ref[:, width:] = dot(columns, grad_value_ref[...], 0, 0).astype(jnp.bfloat16)
 
@@ -198,44 +210,41 @@
     rows, model = memory.shape
     width = grad_keys.shape[1]
     block = model // PEERS
-    steps = RING * RING
     return pl.pallas_call(
         away_body,
         grid_spec=pltpu.PrefetchScalarGridSpec(
             num_scalar_prefetch=1,
-            grid=(steps,),
-            in_specs=[
-                pl.BlockSpec((rows, block), lambda i, table: (0, table[i])),
+            grid=(RING,),
+            in_specs=column_specs(rows, block)
+            + [
                 pl.BlockSpec((rows, width), lambda i, table: (0, 0)),
                 pl.BlockSpec((rows, width), lambda i, table: (0, 0)),
             ],
-            out_specs=pl.BlockSpec((block, 2 * width), lambda i, table: (i, 0)),
+            out_specs=pl.BlockSpec((RING * block, 2 * width), lambda i, table: (i, 0)),
         ),
-        out_shape=jax.ShapeDtypeStruct((steps * block, 2 * width), jnp.bfloat16),
+        out_shape=jax.ShapeDtypeStruct((model // 2, 2 * width), jnp.bfloat16),
         name="away_terms",
-    )(table, memory, grad_keys, grad_values)
-
-
-def home_body(table_ref, memory_ref, grad_key_ref, grad_value_ref, other_ref, *out_refs):
+    )(table, *([memory] * RING), grad_keys, grad_values)
+
+
+def home_body(table_ref, *refs):
     del table_ref
+    grad_key_ref, grad_value_ref, other_ref = refs[RING : RING + 3]
+    out_refs = refs[RING + 3 :]
     y_step = pl.program_id(0)
-    x_step = pl.program_id(1)
     width = grad_key_ref.shape[1]
-    half = other_ref.shape[0] // 2
-    columns = memory_ref[...]
+    half = out_refs[0].shape[1]
+    columns = joined_columns(refs[:RING])
     for start, grad_ref in ((0, grad_key_ref), (width, grad_value_ref)):
         total = dot(columns, grad_ref[...], 0, 0)
         total += other_ref[:, start : start + width].astype(jnp.float32)
-        total = total.astype(jnp.bfloat16)
+        total = total.astype(jnp.bfloat16).reshape(RING, 2 * half, width)
         for step in range(RING):
+            out_refs[RING + step][y_step, :, start : start + width] = total[step, half:]
 
             @pl.when(y_step == step)
             def _():
-                out_refs[step][x_step, :, start : start + width] = total[:half]
-
-            @pl.when(x_step == step)
-            def _():
-                out_refs[RING + step][y_step, :, start : start + width] = total[half:]
+                out_refs[step][:, :, start : start + width] = total[:, :half]
 
 
 def home_terms(table, memory, grad_keys, grad_values, other):
@@ -247,18 +256,18 @@
         home_body,
         grid_spec=pltpu.PrefetchScalarGridSpec(
             num_scalar_prefetch=1,
-            grid=(RING, RING),
-            in_specs=[
-                pl.BlockSpec((rows, block), lambda i, j, table: (0, table[i * RING + j])),
-                pl.BlockSpec((rows, width), lambda i, j, table: (0, 0)),
-                pl.BlockSpec((rows, width), lambda i, j, table: (0, 0)),
-                pl.BlockSpec((block, 2 * width), lambda i, j, table: (i * RING + j, 0)),
+            grid=(RING,),
+            in_specs=column_specs(rows, block)
+            + [
+                pl.BlockSpec((rows, width), lambda i, table: (0, 0)),
+                pl.BlockSpec((rows, width), lambda i, table: (0, 0)),
+                pl.BlockSpec((RING * block, 2 * width), lambda i, table: (i, 0)),
             ],
-            out_specs=[pl.BlockSpec(piece, lambda i, j, table: (0, 0, 0))] * (2 * RING),
+            out_specs=[pl.BlockSpec(piece, lambda i, table: (0, 0, 0))] * (2 * RING),
         ),
         out_shape=[jax.ShapeDtypeStruct(piece, jnp.bfloat16)] * (2 * RING),
         name="home_terms",
-    )(table, memory, grad_keys, grad_values, other)
+    )(table, *([memory] * RING), grad_keys, grad_values, other)
 
 
 def sum_pieces(pieces):
@@ -283,38 +292,29 @@
     ]
 
 
-def memory_body(group_ref, grad_key_ref, grad_value_ref, weight_ref, *refs):
-    out_refs, total_ref = refs[:-1], refs[-1]
+def memory_body(grad_key_ref, grad_value_ref, weight_ref, out_ref):
     width = grad_key_ref.shape[1]
-    rows = out_refs[0].shape[0]
     total = dot(grad_key_ref[...], weight_ref[:, :width], 1, 1)
     total += dot(grad_value_ref[...], weight_ref[:, width:], 1, 1)
-    total_ref[...] = total
-    for step, out_ref in enumerate(out_refs):
-        start = pl.multiple_of((group_ref[0] + step) % RING * rows, rows)
-        out_ref[...] = total_ref[pl.ds(start, rows), :].astype(jnp.bfloat16)
-
-
-def memory_terms(group, grad_keys, grad_values, weights):
+    out_ref[...] = total.astype(jnp.bfloat16)
+
+
+def memory_terms(grad_keys, grad_values, weights):
     rows, width = grad_keys.shape
     model = weights.shape[0]
     block = 512
     return pl.pallas_call(
         memory_body,
-        grid_spec=pltpu.PrefetchScalarGridSpec(
-            num_scalar_prefetch=1,
-            grid=(model // block,),
-            in_specs=[
-                pl.BlockSpec((rows, width), lambda i, group: (0, 0)),
-                pl.BlockSpec((rows, width), lambda i, group: (0, 0)),
-                pl.BlockSpec((block, 2 * width), lambda i, group: (i, 0)),
-            ],
-            out_specs=[pl.BlockSpec((rows // RING, block), lambda i, group: (0, i))] * RING,
-            scratch_shapes=[pltpu.VMEM((rows, block), jnp.float32)],
-        ),
-        out_shape=[jax.ShapeDtypeStruct((rows // RING, model), jnp.bfloat16)] * RING,
+        grid=(model // block,),
+        in_specs=[
+            pl.BlockSpec((rows, width), lambda i: (0, 0)),
+            pl.BlockSpec((rows, width), lambda i: (0, 0)),
+            pl.BlockSpec((block, 2 * width), lambda i: (i, 0)),
+        ],
+        out_specs=pl.BlockSpec((rows, block), lambda i: (0, i)),
+        out_shape=jax.ShapeDtypeStruct((rows, model), jnp.bfloat16),
         name="memory_terms",
-    )(group, grad_keys, grad_values, weights)
+    )(grad_keys, grad_values, weights)
 
 
 def per_device(
@@ -346,14 +346,10 @@
     core = my_index % 2
     away = away_terms(relative_table(1 - core), memory, grad_keys, grad_values)
     other = lax.ppermute(away, "dp", shift(0, 0, 1))
-    group = lax.axis_index("fsdp").astype(jnp.int32).reshape(1)
-    terms = memory_terms(group, grad_keys, grad_values, weights)
+    terms = memory_terms(grad_keys, grad_values, weights)
     other, terms = lax.optimization_barrier((other, terms))
     pieces = home_terms(relative_table(core), memory, grad_keys, grad_values, other)
-    arrived_terms = [terms[0]] + [
-        lax.ppermute(terms[step], "fsdp", [(i, (i + step) % RING) for i in range(RING)])
-        for step in range(1, RING)
-    ]
+    grad_memory = lax.psum_scatter(terms, "fsdp", scatter_dimension=0, tiled=True)
     context, grad_query = unpack_slots(slots, returned)
     sums_y = first_sums(ring_exchange(pieces[:RING], True))
     sums_x = first_sums(ring_exchange(pieces[RING:], False))
@@ -364,7 +360,6 @@
         ],
         axis=0,
     )
-    grad_memory = sum_pieces(arrived_terms).astype(jnp.bfloat16)
     return (
         context,
         grad_query,

time: 242 us -> 207 us (0.86)
  Pallas kernels: 59.8 us -> 45.8 us
  waiting for transfers between devices: 93.8 us -> 84.2 us
  starting transfers between devices: 39.8 us -> 34.4 us
  other arithmetic: 16 us -> 12.1 us
    ppermute x3 -> x0, waiting for transfers between devices: 14 us -> none  [per_device(): lax.ppermute(terms[step], 'fsdp', [(i, (i + step) % RING) for i in range(...]
    pallas_call x1, Pallas kernels: 17.1 us -> 9.29 us  [home_terms(): pl.pallas_call(home_body, grid_spec=pltpu.PrefetchScalarGridSpec(num_scal...]
    pallas_call x1, Pallas kernels: 13.1 us -> 7 us  [away_terms(): pl.pallas_call(away_body, grid_spec=pltpu.PrefetchScalarGridSpec(num_scal...]
    ppermute x3 -> x0, starting transfers between devices: 5.78 us -> none  [per_device(): lax.ppermute(terms[step], 'fsdp', [(i, (i + step) % RING) for i in range(...]
    ppermute x12, waiting for transfers between devices: 22.3 us -> 26.8 us  [ring_exchange(): received.append(lax.ppermute(pieces[step], 'dp', perm))]
    convert_element_type x1 -> x0, other arithmetic: 3.17 us -> none  [per_device(): grad_memory = sum_pieces(arrived_terms).astype(jnp.bfloat16)]
  transfers between devices with their start and end apart: 19 -> 17, of which waited for: 7 -> 7; matrix products, arithmetic and copies ran while one was open for 10% -> 11% of each run, Pallas kernels for 15% -> 13%
where the time goes in v4:
time: 207 us; the launch traced here: 206 us
  waiting for transfers between devices  84.2 us (41%)
  Pallas kernels  45.8 us (22%)
  starting transfers between devices  34.4 us (17%)
  between operations  14.2 us (7%)
  other arithmetic  12.1 us (6%)
  matrix products  10.1 us (5%)
  local copies, waits for them, and re-layouts  5.15 us (2%)
    all_gather x1, waiting for transfers between devices, per_device(): weights = lax.all_gather(stacked, 'dp', axis=0, tiled=True)  57.4 us
    ppermute x12, waiting for transfers between devices, ring_exchange(): received.append(lax.ppermute(pieces[step], 'dp', perm))  26.8 us
    ppermute x12, starting transfers between devices, ring_exchange(): received.append(lax.ppermute(pieces[step], 'dp', perm))  21.2 us
    pallas_call x1, Pallas kernels, attend(): pl.pallas_call(attend_body, grid=(heads, PEERS // BLOCK_PEERS), in_specs=...  11.1 us
    pallas_call x1, Pallas kernels, memory_terms(): pl.pallas_call(memory_body, grid=(model // block,), in_specs=[pl.BlockSpe...  10.6 us
    dot_general x1, matrix products, dot(): lax.dot_general(left, right, (((left_dim,), (right_dim,)), ((), ())), pre...  10.1 us
    pallas_call x1, Pallas kernels, home_terms(): pl.pallas_call(home_body, grid_spec=pltpu.PrefetchScalarGridSpec(num_scal...  9.29 us
    all_to_all x1, starting transfers between devices, per_device(): lax.all_to_all(outgoing, 'dp', split_axis=0, concat_axis=0, tiled=True)  7.4 us
  transfers between devices with their start and end apart: 17, of which 7 were waited for; matrix products, arithmetic and copies ran while one was open for 11% of the time, Pallas kernels for 13%

profile of v4, /device:TPU:0, one launch (start us, length us, event | category | flops | bytes accessed | tf_op | source)
XLA Modules:
  0.0 205.9 jit_solution(8650265048953395806)
XLA Ops:
  7.2 1.7 pad_maximum_fusion.1
  12.0 4.2 %pack_slots.1 = bf16[32,2,32,512]{3,2,1,0:T(8,128)(2,1)} custom-call(s32[1,512]{1,0:T(1,128)} %add_subtract_fusion.slot_ref, bf16[512,512]{1,0:T(8,128)(2,1)} %query_ref.1, bf16[512,512]{1,0:T(8,128)(2,1)} %grad_ref.1), custom_call_target="tpu_custom_call" | custom-call | tf_op jit(solution)/shard_map/pack_slots/pallas_call | solution.py:47
  16.3 7.4 %all-to-all-start = ((bf16[32,2,32,512]{3,2,1,0:T(8,128)(2,1)}), bf16[32,2,32,512]{3,2,1,0:T(8,128)(2,1)S(1)}, u32[]{:S(2)}, u32[]{:S(2)}) async-start(bf16[32,2,32,512]{3,2,1,0:T(8,128)(2,1)} %pack_slots.1), calls=%async_computation | async-start | bytes 4194304 | tf_op jit(solution)/shard_map/all_to_all | solution.py:338
  26.0 57.4 %all-gather.2.cloned.1.call-done.weight_ref = bf16[4096,1024]{1,0:T(8,128)(2,1)} async-done(((bf16[128,1024]{1,0:T(8,128)(2,1)}), bf16[4096,1024]{1,0:T(8,128)(2,1)}) %all-gather.2.cloned.1.call-update) | async-done | bytes 8388624 | tf_op jit(solution)/shard_map/all_gather | solution.py:334
  83.4 10.1 %fusion.key_ref.value_ref = bf16[512,1024]{1,0:T(8,128)(2,1)} fusion(bf16[512,4096]{1,0:T(8,128)(2,1)} %refs_3_.3, bf16[4096,1024]{1,0:T(8,128)(2,1)} %all-gather.2.cloned.1.call-done.weight_ref), kind=kOutput, calls=%fused_computation.1 | convolution fusion | flops 4295491584 | bytes 13631488 | tf_op jit(solution)/shard_map/dot_general | solution.py:20
  94.9 11.1 %attend.1 = (bf16[32,2,32,512]{3,2,1,0:T(8,128)(2,1)}, bf16[512,512]{1,0:T(8,128)(2,1)}, bf16[512,512]{1,0:T(8,128)(2,1)}) custom-call(s32[1024,1]{1,0:T(8,128)} %reshape.134.wanted_ref, s32[1,512]{1,0:T(1,128)} %segment_ref.1, bf16[32,2,32,512]{3,2,1,0:T(8,128)(2,1)} %copy-done, bf16[512,1024]{1,0:T(8,128)(2,1)} %fusion.key_ref.value_ref, ...), custom_call_target="tpu_custom_call" | custom-call | tf_op jit(solution)/shard_map/attend/pallas_call | solution.py:145
  106.0 7.0 %away_terms.1 = bf16[2048,1024]{1,0:T(8,128)(2,1)} custom-call(s32[16]{0:T(128)} %get-tuple-element.45.table_ref, bf16[512,4096]{1,0:T(8,128)(2,1)} %refs_3_.3, bf16[512,4096]{1,0:T(8,128)(2,1)} %refs_3_.3, bf16[512,4096]{1,0:T(8,128)(2,1)} %refs_3_.3, bf16[512,4096]{1,0:T(8,128)(2,1)} %refs_3_.3, bf16[512,512]{1,0:T(8,128)(2,1)} %get-tuple-element.23.refs_4_.grad_key_ref, ...), custom_call_target="tpu_custom_call" | custom-call | tf_op jit(solution)/shard_map/away_terms/pallas_call | solution.py:213
  113.2 10.6 %memory_terms.1 = bf16[512,4096]{1,0:T(8,128)(2,1)} custom-call(bf16[512,512]{1,0:T(8,128)(2,1)} %get-tuple-element.23.refs_4_.grad_key_ref, bf16[512,512]{1,0:T(8,128)(2,1)} %get-tuple-element.24.refs_5_.grad_value_ref, bf16[4096,1024]{1,0:T(8,128)(2,1)} %all-gather.2.cloned.1.call-done.weight_ref), custom_call_target="tpu_custom_call" | custom-call | tf_op jit(solution)/shard_map/memory_terms/pallas_call | solution.py:306
  123.8 5.5 %all-to-all-start.1 = ((bf16[32,2,32,512]{3,2,1,0:T(8,128)(2,1)}), bf16[32,2,32,512]{3,2,1,0:T(8,128)(2,1)S(1)}, u32[]{:S(2)}, u32[]{:S(2)}) async-start(bf16[32,2,32,512]{3,2,1,0:T(8,128)(2,1)} %get-tuple-element.20), calls=%async_computation.1 | async-start | bytes 4194304 | tf_op jit(solution)/shard_map/all_to_all | solution.py:345
  129.3 9.3 %home_terms.1 = (bf16[4,64,1024]{2,1,0:T(8,128)(2,1)}, bf16[4,64,1024]{2,1,0:T(8,128)(2,1)}, bf16[4,64,1024]{2,1,0:T(8,128)(2,1)}, bf16[4,64,1024]{2,1,0:T(8,128...) custom-call(s32[16]{0:T(128)} %get-tuple-element.46.table_ref, ...), custom_call_target="tpu_custom_call" | custom-call | tf_op jit(solution)/shard_map/home_terms/pallas_call | solution.py:255
  138.6 1.8 collective-permute-start.1
  140.4 2.7 %collective-permute-start.2 = (bf16[4,64,1024]{2,1,0:T(8,128)(2,1)}, bf16[4,64,1024]{2,1,0:T(8,128)(2,1)}, u32[]{:S(2)}, u32[]{:S(2)}) collective-permute-start(bf16[4,64,1024]{2,1,0:T(8,128)(2,1)} %get-tuple-element.28), channel_id=1, source_target_pairs={{0,64},{4,68},{8,72},{12,76},{16,80},{20,84},{24,88},{28,92},{32,9... | collective-permute-start | bytes 1572872 | tf_op jit(solution)/shard_map/ppermute | solution.py:284
  146.1 2.7 %collective-permute-start.8 = (bf16[4,64,1024]{2,1,0:T(8,128)(2,1)}, bf16[4,64,1024]{2,1,0:T(8,128)(2,1)}, u32[]{:S(2)}, u32[]{:S(2)}) collective-permute-start(bf16[4,64,1024]{2,1,0:T(8,128)(2,1)} %get-tuple-element.32), channel_id=1, source_target_pairs={{0,16},{4,20},{8,24},{12,28},{16,0},{20,4},{24,8},{28,12},{32,48},... | collective-permute-start | bytes 1572872 | tf_op jit(solution)/shard_map/ppermute | solution.py:284
  148.7 18.5 %collective-permute-done.1 = bf16[4,64,1024]{2,1,0:T(8,128)(2,1)S(1)} collective-permute-done((bf16[4,64,1024]{2,1,0:T(8,128)(2,1)}, bf16[4,64,1024]{2,1,0:T(8,128)(2,1)S(1)}, u32[]{:S(2)}, u32[]{:S(2)}) %collective-permute-start.1) | collective-permute-done | bytes 524320 | tf_op jit(solution)/shard_map/ppermute | solution.py:284
  167.3 2.6 %collective-permute-start.9 = (bf16[4,64,1024]{2,1,0:T(8,128)(2,1)}, bf16[4,64,1024]{2,1,0:T(8,128)(2,1)}, u32[]{:S(2)}, u32[]{:S(2)}) collective-permute-start(bf16[4,64,1024]{2,1,0:T(8,128)(2,1)} %get-tuple-element.33), channel_id=1, source_target_pairs={{0,24},{4,28},{8,0},{12,4},{16,8},{20,12},{24,16},{28,20},{32,56},... | collective-permute-start | bytes 1572872 | tf_op jit(solution)/shard_map/ppermute | solution.py:284
  172.3 3.6 %unpack_slots.1 = (bf16[512,512]{1,0:T(8,128)(2,1)}, bf16[512,512]{1,0:T(8,128)(2,1)}) custom-call(s32[512,1]{1,0:T(8,128)} %sub.36.slot_ref, bf16[32,2,32,512]{3,2,1,0:T(8,128)(2,1)} %copy-done.1), custom_call_target="tpu_custom_call" | custom-call | tf_op jit(solution)/shard_map/unpack_slots/pallas_call | solution.py:74
  175.9 3.0 %collective-permute-done.2 = bf16[4,64,1024]{2,1,0:T(8,128)(2,1)} collective-permute-done((bf16[4,64,1024]{2,1,0:T(8,128)(2,1)}, bf16[4,64,1024]{2,1,0:T(8,128)(2,1)}, u32[]{:S(2)}, u32[]{:S(2)}) %collective-permute-start.2) | collective-permute-done | bytes 524320 | tf_op jit(solution)/shard_map/ppermute | solution.py:284
  178.9 1.7 fusion.7
  180.6 1.6 collective-permute-start.4
  182.2 1.9 collective-permute-start.6
  184.1 1.6 collective-permute-start.5
  187.4 3.2 %collective-permute-start.12 = (bf16[64,1024]{1,0:T(8,128)(2,1)S(1)}, bf16[64,1024]{1,0:T(8,128)(2,1)S(1)}, u32[]{:S(2)}, u32[]{:S(2)}) collective-permute-start(bf16[64,1024]{1,0:T(8,128)(2,1)S(1)} %get-tuple-element.38), channel_id=1, source_target_pairs={{0,96},{4,100},{8,104},{12,108},{16,112},{20,116},{24,120},{28,124... | collective-permute-start | bytes 393224 | tf_op jit(solution)/shard_map/ppermute | solution.py:284
  192.2 2.8 %collective-permute-done.10 = bf16[64,1024]{1,0:T(8,128)(2,1)S(1)} collective-permute-done((bf16[64,1024]{1,0:T(8,128)(2,1)S(1)}, bf16[64,1024]{1,0:T(8,128)(2,1)S(1)}, u32[]{:S(2)}, u32[]{:S(2)}) %collective-permute-start.10) | collective-permute-done | bytes 131104 | tf_op jit(solution)/shard_map/ppermute | solution.py:284
  195.3 1.8 collective-permute-done.11
  (52 shorter events, 17.9 us)
Async XLA Ops:
  7.2 16.6 %copy-start.4 = (s32[32,32]{1,0:T(8,128)S(1)}, s32[32,32]{1,0:T(8,128)}, u32[]{:S(2)}) copy-start(s32[32,32]{1,0:T(8,128)} %param.16) | copy-start | bytes 12292
  7.2 16.6 %copy-start.5 = (s32[32,32]{1,0:T(8,128)S(1)}, s32[32,32]{1,0:T(8,128)}, u32[]{:S(2)}) copy-start(s32[32,32]{1,0:T(8,128)} %param.17) | copy-start | bytes 12292
  7.2 76.2 %all-gather.2.cloned.1.call-start = ((), (), s32[]{:S(2)}) async-start(), calls=%async_computation.3 | async-start | bytes 8650752 | tf_op jit(solution)/shard_map/all_gather | solution.py:334
  16.3 77.2 %all-to-all-start = ((bf16[32,2,32,512]{3,2,1,0:T(8,128)(2,1)}), bf16[32,2,32,512]{3,2,1,0:T(8,128)(2,1)S(1)}, u32[]{:S(2)}, u32[]{:S(2)}) async-start(bf16[32,2,32,512]{3,2,1,0:T(8,128)(2,1)} %pack_slots.1), calls=%async_computation | async-start | bytes 4194304 | tf_op jit(solution)/shard_map/all_to_all | solution.py:338
  23.7 175.4 %reduce-scatter.2.cloned.1.call-start = ((), (), s32[]{:S(2)}) async-start(), calls=%async_computation.4 | async-start | bytes 5242880 | tf_op jit(solution)/shard_map/reduce_scatter | solution.py:352
  93.5 1.4 copy-start
  113.0 10.8 %collective-permute-start = (bf16[2048,1024]{1,0:T(8,128)(2,1)}, bf16[2048,1024]{1,0:T(8,128)(2,1)}, u32[]{:S(2)}, u32[]{:S(2)}) collective-permute-start(bf16[2048,1024]{1,0:T(8,128)(2,1)} %away_terms.1), channel_id=1, source_target_pairs={{0,4},{4,0},{8,12},{12,8},{16,20},{20,16},{24,28},{28,24},{32,36},... | collective-permute-start | bytes 12582920 | tf_op jit(solution)/shard_map/ppermute | solution.py:348
  123.8 47.1 %all-to-all-start.1 = ((bf16[32,2,32,512]{3,2,1,0:T(8,128)(2,1)}), bf16[32,2,32,512]{3,2,1,0:T(8,128)(2,1)S(1)}, u32[]{:S(2)}, u32[]{:S(2)}) async-start(bf16[32,2,32,512]{3,2,1,0:T(8,128)(2,1)} %get-tuple-element.20), calls=%async_computation.1 | async-start | bytes 4194304 | tf_op jit(solution)/shard_map/all_to_all | solution.py:345
  138.6 47.1 %copy-start.2 = (bf16[4,64,1024]{2,1,0:T(8,128)(2,1)S(1)}, bf16[4,64,1024]{2,1,0:T(8,128)(2,1)}, u32[]{:S(2)}) copy-start(bf16[4,64,1024]{2,1,0:T(8,128)(2,1)} %get-tuple-element.30) | copy-start | bytes 1572868
  138.6 28.7 %collective-permute-start.1 = (bf16[4,64,1024]{2,1,0:T(8,128)(2,1)}, bf16[4,64,1024]{2,1,0:T(8,128)(2,1)S(1)}, u32[]{:S(2)}, u32[]{:S(2)}) collective-permute-start(bf16[4,64,1024]{2,1,0:T(8,128)(2,1)} %get-tuple-element.27), channel_id=1, source_target_pairs={{0,32},{4,36},{8,40},{12,44},{16,48},{20,52},{24,56},{28,60},{32,6... | collective-permute-start | bytes 1572872 | tf_op jit(solution)/shard_map/ppermute | solution.py:284
  140.4 38.4 %collective-permute-start.2 = (bf16[4,64,1024]{2,1,0:T(8,128)(2,1)}, bf16[4,64,1024]{2,1,0:T(8,128)(2,1)}, u32[]{:S(2)}, u32[]{:S(2)}) collective-permute-start(bf16[4,64,1024]{2,1,0:T(8,128)(2,1)} %get-tuple-element.28), channel_id=1, source_target_pairs={{0,64},{4,68},{8,72},{12,76},{16,80},{20,84},{24,88},{28,92},{32,9... | collective-permute-start | bytes 1572872 | tf_op jit(solution)/shard_map/ppermute | solution.py:284
  143.2 35.7 %collective-permute-start.3 = (bf16[4,64,1024]{2,1,0:T(8,128)(2,1)}, bf16[4,64,1024]{2,1,0:T(8,128)(2,1)}, u32[]{:S(2)}, u32[]{:S(2)}) collective-permute-start(bf16[4,64,1024]{2,1,0:T(8,128)(2,1)} %get-tuple-element.29), channel_id=1, source_target_pairs={{0,96},{4,100},{8,104},{12,108},{16,112},{20,116},{24,120},{28,124... | collective-permute-start | bytes 1572872 | tf_op jit(solution)/shard_map/ppermute | solution.py:284
  144.6 39.5 %collective-permute-start.7 = (bf16[4,64,1024]{2,1,0:T(8,128)(2,1)}, bf16[4,64,1024]{2,1,0:T(8,128)(2,1)}, u32[]{:S(2)}, u32[]{:S(2)}) collective-permute-start(bf16[4,64,1024]{2,1,0:T(8,128)(2,1)} %get-tuple-element.31), channel_id=1, source_target_pairs={{0,8},{4,12},{8,16},{12,20},{16,24},{20,28},{24,0},{28,4},{32,40},... | collective-permute-start | bytes 1572872 | tf_op jit(solution)/shard_map/ppermute | solution.py:284
  146.1 39.7 %collective-permute-start.8 = (bf16[4,64,1024]{2,1,0:T(8,128)(2,1)}, bf16[4,64,1024]{2,1,0:T(8,128)(2,1)}, u32[]{:S(2)}, u32[]{:S(2)}) collective-permute-start(bf16[4,64,1024]{2,1,0:T(8,128)(2,1)} %get-tuple-element.32), channel_id=1, source_target_pairs={{0,16},{4,20},{8,24},{12,28},{16,0},{20,4},{24,8},{28,12},{32,48},... | collective-permute-start | bytes 1572872 | tf_op jit(solution)/shard_map/ppermute | solution.py:284
  167.3 2.6 %copy-start.3 = (bf16[4,64,1024]{2,1,0:T(8,128)(2,1)}, bf16[4,64,1024]{2,1,0:T(8,128)(2,1)S(1)}, u32[]{:S(2)}) copy-start(bf16[4,64,1024]{2,1,0:T(8,128)(2,1)S(1)} %collective-permute-done.1) | copy-start | bytes 1572868
  167.3 18.5 %collective-permute-start.9 = (bf16[4,64,1024]{2,1,0:T(8,128)(2,1)}, bf16[4,64,1024]{2,1,0:T(8,128)(2,1)}, u32[]{:S(2)}, u32[]{:S(2)}) collective-permute-start(bf16[4,64,1024]{2,1,0:T(8,128)(2,1)} %get-tuple-element.33), channel_id=1, source_target_pairs={{0,24},{4,28},{8,0},{12,4},{16,8},{20,12},{24,16},{28,20},{32,56},... | collective-permute-start | bytes 1572872 | tf_op jit(solution)/shard_map/ppermute | solution.py:284
  170.9 1.3 copy-start.1
  180.6 10.0 %collective-permute-start.4 = (bf16[64,1024]{1,0:T(8,128)(2,1)S(1)}, bf16[64,1024]{1,0:T(8,128)(2,1)S(1)}, u32[]{:S(2)}, u32[]{:S(2)}) collective-permute-start(bf16[64,1024]{1,0:T(8,128)(2,1)S(1)} %get-tuple-element.40), channel_id=1, source_target_pairs={{0,8},{4,12},{8,16},{12,20},{16,24},{20,28},{24,0},{28,4},{32,40},... | collective-permute-start | bytes 393224 | tf_op jit(solution)/shard_map/ppermute | solution.py:284
  182.2 8.5 %collective-permute-start.6 = (bf16[64,1024]{1,0:T(8,128)(2,1)S(1)}, bf16[64,1024]{1,0:T(8,128)(2,1)S(1)}, u32[]{:S(2)}, u32[]{:S(2)}) collective-permute-start(bf16[64,1024]{1,0:T(8,128)(2,1)S(1)} %get-tuple-element.41), channel_id=1, source_target_pairs={{0,24},{4,28},{8,0},{12,4},{16,8},{20,12},{24,16},{28,20},{32,56},... | collective-permute-start | bytes 393224 | tf_op jit(solution)/shard_map/ppermute | solution.py:284
  184.1 6.9 %collective-permute-start.5 = (bf16[64,1024]{1,0:T(8,128)(2,1)S(1)}, bf16[64,1024]{1,0:T(8,128)(2,1)S(1)}, u32[]{:S(2)}, u32[]{:S(2)}) collective-permute-start(bf16[64,1024]{1,0:T(8,128)(2,1)S(1)} %get-tuple-element.42), channel_id=1, source_target_pairs={{0,16},{4,20},{8,24},{12,28},{16,0},{20,4},{24,8},{28,12},{32,48},... | collective-permute-start | bytes 393224 | tf_op jit(solution)/shard_map/ppermute | solution.py:284
  187.3 7.7 %collective-permute-start.10 = (bf16[64,1024]{1,0:T(8,128)(2,1)S(1)}, bf16[64,1024]{1,0:T(8,128)(2,1)S(1)}, u32[]{:S(2)}, u32[]{:S(2)}) collective-permute-start(bf16[64,1024]{1,0:T(8,128)(2,1)S(1)} %get-tuple-element.37), channel_id=1, source_target_pairs={{0,32},{4,36},{8,40},{12,44},{16,48},{20,52},{24,56},{28,60},{32,6... | collective-permute-start | bytes 393224 | tf_op jit(solution)/shard_map/ppermute | solution.py:284
  187.4 7.9 %collective-permute-start.12 = (bf16[64,1024]{1,0:T(8,128)(2,1)S(1)}, bf16[64,1024]{1,0:T(8,128)(2,1)S(1)}, u32[]{:S(2)}, u32[]{:S(2)}) collective-permute-start(bf16[64,1024]{1,0:T(8,128)(2,1)S(1)} %get-tuple-element.38), channel_id=1, source_target_pairs={{0,96},{4,100},{8,104},{12,108},{16,112},{20,116},{24,120},{28,124... | collective-permute-start | bytes 393224 | tf_op jit(solution)/shard_map/ppermute | solution.py:284
  190.6 6.5 %collective-permute-start.11 = (bf16[64,1024]{1,0:T(8,128)(2,1)S(1)}, bf16[64,1024]{1,0:T(8,128)(2,1)S(1)}, u32[]{:S(2)}, u32[]{:S(2)}) collective-permute-start(bf16[64,1024]{1,0:T(8,128)(2,1)S(1)} %get-tuple-element.39), channel_id=1, source_target_pairs={{0,64},{4,68},{8,72},{12,76},{16,80},{20,84},{24,88},{28,92},{32,9... | collective-permute-start | bytes 393224 | tf_op jit(solution)/shard_map/ppermute | solution.py:284
Sparse Core Ops, SparseCore 0:
  10.9 72.4 all-gather.1
  124.0 46.6 reduce-scatter.1

commit v5 on v4

--- a/solution.py
+++ b/solution.py
@@ -347,7 +347,7 @@
     away = away_terms(relative_table(1 - core), memory, grad_keys, grad_values)
     other = lax.ppermute(away, "dp", shift(0, 0, 1))
     terms = memory_terms(grad_keys, grad_values, weights)
-    other, terms = lax.optimization_barrier((other, terms))
+    other, terms, returned = lax.optimization_barrier((other, terms, returned))
     pieces = home_terms(relative_table(core), memory, grad_keys, grad_values, other)
     grad_memory = lax.psum_scatter(terms, "fsdp", scatter_dimension=0, tiled=True)
     context, grad_query = unpack_slots(slots, returned)

time: 207 us -> 214 us (1.034)
  waiting for transfers between devices: 84.2 us -> 97.1 us
  starting transfers between devices: 34.4 us -> 31.8 us
  other arithmetic: 12.1 us -> 9.61 us
    all_to_all x1, waiting for transfers between devices: 0.01 us -> 19.3 us  [per_device(): lax.all_to_all(answers, 'dp', split_axis=0, concat_axis=0, tiled=True)]
    ppermute x12, waiting for transfers between devices: 26.8 us -> 20.2 us  [ring_exchange(): received.append(lax.ppermute(pieces[step], 'dp', perm))]
    ppermute x12, starting transfers between devices: 21.2 us -> 18.6 us  [ring_exchange(): received.append(lax.ppermute(pieces[step], 'dp', perm))]
    add x4, other arithmetic: 5.68 us -> 3.14 us  [sum_pieces(): total += piece.astype(jnp.float32)]
  transfers between devices with their start and end apart: 17 -> 17, of which waited for: 7 -> 8; matrix products, arithmetic and copies ran while one was open for 11% -> 10% of each run, Pallas kernels for 13% -> 13%
where the time goes in v5:
time: 214 us; the launch traced here: 212 us
  waiting for transfers between devices  97.1 us (45%)
  Pallas kernels  45.8 us (21%)
  starting transfers between devices  31.8 us (15%)
  between operations  14.2 us (7%)
  matrix products  10.1 us (5%)
  other arithmetic  9.61 us (4%)
  local copies, waits for them, and re-layouts  3.82 us (2%)
    all_gather x1, waiting for transfers between devices, per_device(): weights = lax.all_gather(stacked, 'dp', axis=0, tiled=True)  57.6 us
    ppermute x12, waiting for transfers between devices, ring_exchange(): received.append(lax.ppermute(pieces[step], 'dp', perm))  20.2 us
    all_to_all x1, waiting for transfers between devices, per_device(): lax.all_to_all(answers, 'dp', split_axis=0, concat_axis=0, tiled=True)  19.3 us
    ppermute x12, starting transfers between devices, ring_exchange(): received.append(lax.ppermute(pieces[step], 'dp', perm))  18.6 us
    pallas_call x1, Pallas kernels, attend(): pl.pallas_call(attend_body, grid=(heads, PEERS // BLOCK_PEERS), in_specs=...  11.1 us
    pallas_call x1, Pallas kernels, memory_terms(): pl.pallas_call(memory_body, grid=(model // block,), in_specs=[pl.BlockSpe...  10.7 us
    dot_general x1, matrix products, dot(): lax.dot_general(left, right, (((left_dim,), (right_dim,)), ((), ())), pre...  10.1 us
    pallas_call x1, Pallas kernels, home_terms(): pl.pallas_call(home_body, grid_spec=pltpu.PrefetchScalarGridSpec(num_scal...  9.27 us
  transfers between devices with their start and end apart: 17, of which 8 were waited for; matrix products, arithmetic and copies ran while one was open for 10% of the time, Pallas kernels for 13%

profile of v5, /device:TPU:0, one launch (start us, length us, event | category | flops | bytes accessed | tf_op | source)
XLA Modules:
  0.0 212.5 jit_solution(10433579672217383611)
XLA Ops:
  7.2 1.7 pad_maximum_fusion.1
  12.0 4.2 %pack_slots.1 = bf16[32,2,32,512]{3,2,1,0:T(8,128)(2,1)} custom-call(s32[1,512]{1,0:T(1,128)} %add_subtract_fusion.slot_ref, bf16[512,512]{1,0:T(8,128)(2,1)} %query_ref.1, bf16[512,512]{1,0:T(8,128)(2,1)} %grad_ref.1), custom_call_target="tpu_custom_call" | custom-call | tf_op jit(solution)/shard_map/pack_slots/pallas_call | solution.py:47
  16.2 7.4 %all-to-all-start = ((bf16[32,2,32,512]{3,2,1,0:T(8,128)(2,1)}), bf16[32,2,32,512]{3,2,1,0:T(8,128)(2,1)S(1)}, u32[]{:S(2)}, u32[]{:S(2)}) async-start(bf16[32,2,32,512]{3,2,1,0:T(8,128)(2,1)} %pack_slots.1), calls=%async_computation | async-start | bytes 4194304 | tf_op jit(solution)/shard_map/all_to_all | solution.py:338
  24.0 1.3 reshape.134.wanted_ref
  26.0 57.6 %all-gather.2.cloned.1.call-done.weight_ref = bf16[4096,1024]{1,0:T(8,128)(2,1)} async-done(((bf16[128,1024]{1,0:T(8,128)(2,1)}), bf16[4096,1024]{1,0:T(8,128)(2,1)}) %all-gather.2.cloned.1.call-update) | async-done | bytes 8388624 | tf_op jit(solution)/shard_map/all_gather | solution.py:334
  83.5 10.1 %fusion.key_ref.value_ref = bf16[512,1024]{1,0:T(8,128)(2,1)} fusion(bf16[512,4096]{1,0:T(8,128)(2,1)} %refs_3_.3, bf16[4096,1024]{1,0:T(8,128)(2,1)} %all-gather.2.cloned.1.call-done.weight_ref), kind=kOutput, calls=%fused_computation.1 | convolution fusion | flops 4295491584 | bytes 13631488 | tf_op jit(solution)/shard_map/dot_general | solution.py:20
  93.7 1.4 copy-done
  95.1 11.1 %attend.1 = (bf16[32,2,32,512]{3,2,1,0:T(8,128)(2,1)}, bf16[512,512]{1,0:T(8,128)(2,1)}, bf16[512,512]{1,0:T(8,128)(2,1)}) custom-call(s32[1024,1]{1,0:T(8,128)} %reshape.134.wanted_ref, s32[1,512]{1,0:T(1,128)} %segment_ref.1, bf16[32,2,32,512]{3,2,1,0:T(8,128)(2,1)} %copy-done, bf16[512,1024]{1,0:T(8,128)(2,1)} %fusion.key_ref.value_ref, ...), custom_call_target="tpu_custom_call" | custom-call | tf_op jit(solution)/shard_map/attend/pallas_call | solution.py:145
  106.2 7.0 %away_terms.1 = bf16[2048,1024]{1,0:T(8,128)(2,1)} custom-call(s32[16]{0:T(128)} %get-tuple-element.48.table_ref, bf16[512,4096]{1,0:T(8,128)(2,1)} %refs_3_.3, bf16[512,4096]{1,0:T(8,128)(2,1)} %refs_3_.3, bf16[512,4096]{1,0:T(8,128)(2,1)} %refs_3_.3, bf16[512,4096]{1,0:T(8,128)(2,1)} %refs_3_.3, bf16[512,512]{1,0:T(8,128)(2,1)} %get-tuple-element.21.refs_4_.grad_key_ref, ...), custom_call_target="tpu_custom_call" | custom-call | tf_op jit(solution)/shard_map/away_terms/pallas_call | solution.py:213
  113.4 5.5 %all-to-all-start.1 = ((bf16[32,2,32,512]{3,2,1,0:T(8,128)(2,1)}), bf16[32,2,32,512]{3,2,1,0:T(8,128)(2,1)S(1)}, u32[]{:S(2)}, u32[]{:S(2)}) async-start(bf16[32,2,32,512]{3,2,1,0:T(8,128)(2,1)} %get-tuple-element.23), calls=%async_computation.1 | async-start | bytes 4194304 | tf_op jit(solution)/shard_map/all_to_all | solution.py:345
  118.9 10.7 %memory_terms.1 = bf16[512,4096]{1,0:T(8,128)(2,1)} custom-call(bf16[512,512]{1,0:T(8,128)(2,1)} %get-tuple-element.21.refs_4_.grad_key_ref, bf16[512,512]{1,0:T(8,128)(2,1)} %get-tuple-element.22.refs_5_.grad_value_ref, bf16[4096,1024]{1,0:T(8,128)(2,1)} %all-gather.2.cloned.1.call-done.weight_ref), custom_call_target="tpu_custom_call" | custom-call | tf_op jit(solution)/shard_map/memory_terms/pallas_call | solution.py:306
  129.6 19.3 %all-to-all-done.1.in_ref = bf16[32,2,32,512]{3,2,1,0:T(8,128)(2,1)S(1)} async-done(((bf16[32,2,32,512]{3,2,1,0:T(8,128)(2,1)}), bf16[32,2,32,512]{3,2,1,0:T(8,128)(2,1)S(1)}, u32[]{:S(2)}, u32[]{:S(2)}) %all-to-all-start.1) | async-done | bytes 2097184 | tf_op jit(solution)/shard_map/all_to_all | solution.py:345
  148.9 9.3 %home_terms.1 = (bf16[4,64,1024]{2,1,0:T(8,128)(2,1)}, bf16[4,64,1024]{2,1,0:T(8,128)(2,1)}, bf16[4,64,1024]{2,1,0:T(8,128)(2,1)}, bf16[4,64,1024]{2,1,0:T(8,128...) custom-call(s32[16]{0:T(128)} %get-tuple-element.47.table_ref, ...), custom_call_target="tpu_custom_call" | custom-call | tf_op jit(solution)/shard_map/home_terms/pallas_call | solution.py:255
  158.3 1.9 collective-permute-start.2
  160.1 1.7 collective-permute-start.3
  163.2 10.1 %collective-permute-done.1 = bf16[4,64,1024]{2,1,0:T(8,128)(2,1)S(1)} collective-permute-done((bf16[4,64,1024]{2,1,0:T(8,128)(2,1)}, bf16[4,64,1024]{2,1,0:T(8,128)(2,1)S(1)}, u32[]{:S(2)}, u32[]{:S(2)}) %collective-permute-start.1) | collective-permute-done | bytes 524320 | tf_op jit(solution)/shard_map/ppermute | solution.py:284
  174.3 3.6 %unpack_slots.1 = (bf16[512,512]{1,0:T(8,128)(2,1)}, bf16[512,512]{1,0:T(8,128)(2,1)}) custom-call(s32[512,1]{1,0:T(8,128)} %sub.36.slot_ref, bf16[32,2,32,512]{3,2,1,0:T(8,128)(2,1)} %copy-done.1), custom_call_target="tpu_custom_call" | custom-call | tf_op jit(solution)/shard_map/unpack_slots/pallas_call | solution.py:74
  177.9 5.2 %collective-permute-done.2 = bf16[4,64,1024]{2,1,0:T(8,128)(2,1)} collective-permute-done((bf16[4,64,1024]{2,1,0:T(8,128)(2,1)}, bf16[4,64,1024]{2,1,0:T(8,128)(2,1)}, u32[]{:S(2)}, u32[]{:S(2)}) %collective-permute-start.2) | collective-permute-done | bytes 524320 | tf_op jit(solution)/shard_map/ppermute | solution.py:284
  183.7 1.6 fusion.7
  185.3 5.3 %collective-permute-start.4 = (bf16[64,1024]{1,0:T(8,128)(2,1)S(1)}, bf16[64,1024]{1,0:T(8,128)(2,1)S(1)}, u32[]{:S(2)}, u32[]{:S(2)}) collective-permute-start(bf16[64,1024]{1,0:T(8,128)(2,1)S(1)} %get-tuple-element.42), channel_id=1, source_target_pairs={{0,8},{4,12},{8,16},{12,20},{16,24},{20,28},{24,0},{28,4},{32,40},... | collective-permute-start | bytes 393224 | tf_op jit(solution)/shard_map/ppermute | solution.py:284
  190.5 1.3 collective-permute-start.6
  191.8 2.8 %collective-permute-start.5 = (bf16[64,1024]{1,0:T(8,128)(2,1)S(1)}, bf16[64,1024]{1,0:T(8,128)(2,1)S(1)}, u32[]{:S(2)}, u32[]{:S(2)}) collective-permute-start(bf16[64,1024]{1,0:T(8,128)(2,1)S(1)} %get-tuple-element.44), channel_id=1, source_target_pairs={{0,16},{4,20},{8,24},{12,28},{16,0},{20,4},{24,8},{28,12},{32,48},... | collective-permute-start | bytes 393224 | tf_op jit(solution)/shard_map/ppermute | solution.py:284
  195.0 3.2 %collective-permute-start.12 = (bf16[64,1024]{1,0:T(8,128)(2,1)S(1)}, bf16[64,1024]{1,0:T(8,128)(2,1)S(1)}, u32[]{:S(2)}, u32[]{:S(2)}) collective-permute-start(bf16[64,1024]{1,0:T(8,128)(2,1)S(1)} %get-tuple-element.40), channel_id=1, source_target_pairs={{0,96},{4,100},{8,104},{12,108},{16,112},{20,116},{24,120},{28,124... | collective-permute-start | bytes 393224 | tf_op jit(solution)/shard_map/ppermute | solution.py:284
  202.1 2.6 %collective-permute-done.11 = bf16[64,1024]{1,0:T(8,128)(2,1)S(1)} collective-permute-done((bf16[64,1024]{1,0:T(8,128)(2,1)S(1)}, bf16[64,1024]{1,0:T(8,128)(2,1)S(1)}, u32[]{:S(2)}, u32[]{:S(2)}) %collective-permute-start.11) | collective-permute-done | bytes 131104 | tf_op jit(solution)/shard_map/ppermute | solution.py:284
  (50 shorter events, 12.6 us)
Async XLA Ops:
  7.2 16.5 %copy-start.3 = (s32[32,32]{1,0:T(8,128)S(1)}, s32[32,32]{1,0:T(8,128)}, u32[]{:S(2)}) copy-start(s32[32,32]{1,0:T(8,128)} %param.16) | copy-start | bytes 12292
  7.2 16.5 %copy-start.4 = (s32[32,32]{1,0:T(8,128)S(1)}, s32[32,32]{1,0:T(8,128)}, u32[]{:S(2)}) copy-start(s32[32,32]{1,0:T(8,128)} %param.17) | copy-start | bytes 12292
  7.2 76.4 %all-gather.2.cloned.1.call-start = ((), (), s32[]{:S(2)}) async-start(), calls=%async_computation.3 | async-start | bytes 8650752 | tf_op jit(solution)/shard_map/all_gather | solution.py:334
  16.2 77.4 %all-to-all-start = ((bf16[32,2,32,512]{3,2,1,0:T(8,128)(2,1)}), bf16[32,2,32,512]{3,2,1,0:T(8,128)(2,1)S(1)}, u32[]{:S(2)}, u32[]{:S(2)}) async-start(bf16[32,2,32,512]{3,2,1,0:T(8,128)(2,1)} %pack_slots.1), calls=%async_computation | async-start | bytes 4194304 | tf_op jit(solution)/shard_map/all_to_all | solution.py:338
  93.7 1.4 copy-start
  113.2 35.7 %collective-permute-start = (bf16[2048,1024]{1,0:T(8,128)(2,1)}, bf16[2048,1024]{1,0:T(8,128)(2,1)}, u32[]{:S(2)}, u32[]{:S(2)}) collective-permute-start(bf16[2048,1024]{1,0:T(8,128)(2,1)} %away_terms.1), channel_id=1, source_target_pairs={{0,4},{4,0},{8,12},{12,8},{16,20},{20,16},{24,28},{28,24},{32,36},... | collective-permute-start | bytes 12582920 | tf_op jit(solution)/shard_map/ppermute | solution.py:348
  113.4 35.5 %all-to-all-start.1 = ((bf16[32,2,32,512]{3,2,1,0:T(8,128)(2,1)}), bf16[32,2,32,512]{3,2,1,0:T(8,128)(2,1)S(1)}, u32[]{:S(2)}, u32[]{:S(2)}) async-start(bf16[32,2,32,512]{3,2,1,0:T(8,128)(2,1)} %get-tuple-element.23), calls=%async_computation.1 | async-start | bytes 4194304 | tf_op jit(solution)/shard_map/all_to_all | solution.py:345
  118.9 86.7 %reduce-scatter.2.cloned.1.call-start = ((), (), s32[]{:S(2)}) async-start(), calls=%async_computation.4 | async-start | bytes 5242880 | tf_op jit(solution)/shard_map/reduce_scatter | solution.py:352
  148.9 9.3 %copy-start.1 = (bf16[32,2,32,512]{3,2,1,0:T(8,128)(2,1)}, bf16[32,2,32,512]{3,2,1,0:T(8,128)(2,1)S(1)}, u32[]{:S(2)}) copy-start(bf16[32,2,32,512]{3,2,1,0:T(8,128)(2,1)S(1)} %all-to-all-done.1.in_ref) | copy-start | bytes 6291460
  158.2 36.4 %copy-start.2 = (bf16[4,64,1024]{2,1,0:T(8,128)(2,1)S(1)}, bf16[4,64,1024]{2,1,0:T(8,128)(2,1)}, u32[]{:S(2)}) copy-start(bf16[4,64,1024]{2,1,0:T(8,128)(2,1)} %get-tuple-element.32) | copy-start | bytes 1572868
  158.2 15.1 %collective-permute-start.1 = (bf16[4,64,1024]{2,1,0:T(8,128)(2,1)}, bf16[4,64,1024]{2,1,0:T(8,128)(2,1)S(1)}, u32[]{:S(2)}, u32[]{:S(2)}) collective-permute-start(bf16[4,64,1024]{2,1,0:T(8,128)(2,1)} %get-tuple-element.29), channel_id=1, source_target_pairs={{0,32},{4,36},{8,40},{12,44},{16,48},{20,52},{24,56},{28,60},{32,6... | collective-permute-start | bytes 1572872 | tf_op jit(solution)/shard_map/ppermute | solution.py:284
  158.3 24.8 %collective-permute-start.2 = (bf16[4,64,1024]{2,1,0:T(8,128)(2,1)}, bf16[4,64,1024]{2,1,0:T(8,128)(2,1)}, u32[]{:S(2)}, u32[]{:S(2)}) collective-permute-start(bf16[4,64,1024]{2,1,0:T(8,128)(2,1)} %get-tuple-element.30), channel_id=1, source_target_pairs={{0,64},{4,68},{8,72},{12,76},{16,80},{20,84},{24,88},{28,92},{32,9... | collective-permute-start | bytes 1572872 | tf_op jit(solution)/shard_map/ppermute | solution.py:284
  160.1 23.6 %collective-permute-start.3 = (bf16[4,64,1024]{2,1,0:T(8,128)(2,1)}, bf16[4,64,1024]{2,1,0:T(8,128)(2,1)}, u32[]{:S(2)}, u32[]{:S(2)}) collective-permute-start(bf16[4,64,1024]{2,1,0:T(8,128)(2,1)} %get-tuple-element.31), channel_id=1, source_target_pairs={{0,96},{4,100},{8,104},{12,108},{16,112},{20,116},{24,120},{28,124... | collective-permute-start | bytes 1572872 | tf_op jit(solution)/shard_map/ppermute | solution.py:284
  161.9 30.0 %collective-permute-start.7 = (bf16[4,64,1024]{2,1,0:T(8,128)(2,1)}, bf16[4,64,1024]{2,1,0:T(8,128)(2,1)S(1)}, u32[]{:S(2)}, u32[]{:S(2)}) collective-permute-start(bf16[4,64,1024]{2,1,0:T(8,128)(2,1)} %get-tuple-element.33), channel_id=1, source_target_pairs={{0,8},{4,12},{8,16},{12,20},{16,24},{20,28},{24,0},{28,4},{32,40},... | collective-permute-start | bytes 1572872 | tf_op jit(solution)/shard_map/ppermute | solution.py:284
  161.9 32.7 %collective-permute-start.8 = (bf16[4,64,1024]{2,1,0:T(8,128)(2,1)}, bf16[4,64,1024]{2,1,0:T(8,128)(2,1)S(1)}, u32[]{:S(2)}, u32[]{:S(2)}) collective-permute-start(bf16[4,64,1024]{2,1,0:T(8,128)(2,1)} %get-tuple-element.34), channel_id=1, source_target_pairs={{0,16},{4,20},{8,24},{12,28},{16,0},{20,4},{24,8},{28,12},{32,48},... | collective-permute-start | bytes 1572872 | tf_op jit(solution)/shard_map/ppermute | solution.py:284
  173.3 21.4 %collective-permute-start.9 = (bf16[4,64,1024]{2,1,0:T(8,128)(2,1)}, bf16[4,64,1024]{2,1,0:T(8,128)(2,1)S(1)}, u32[]{:S(2)}, u32[]{:S(2)}) collective-permute-start(bf16[4,64,1024]{2,1,0:T(8,128)(2,1)} %get-tuple-element.35), channel_id=1, source_target_pairs={{0,24},{4,28},{8,0},{12,4},{16,8},{20,12},{24,16},{28,20},{32,56},... | collective-permute-start | bytes 1572872 | tf_op jit(solution)/shard_map/ppermute | solution.py:284
  185.3 12.9 %collective-permute-start.4 = (bf16[64,1024]{1,0:T(8,128)(2,1)S(1)}, bf16[64,1024]{1,0:T(8,128)(2,1)S(1)}, u32[]{:S(2)}, u32[]{:S(2)}) collective-permute-start(bf16[64,1024]{1,0:T(8,128)(2,1)S(1)} %get-tuple-element.42), channel_id=1, source_target_pairs={{0,8},{4,12},{8,16},{12,20},{16,24},{20,28},{24,0},{28,4},{32,40},... | collective-permute-start | bytes 393224 | tf_op jit(solution)/shard_map/ppermute | solution.py:284
  190.5 8.7 %collective-permute-start.6 = (bf16[64,1024]{1,0:T(8,128)(2,1)S(1)}, bf16[64,1024]{1,0:T(8,128)(2,1)S(1)}, u32[]{:S(2)}, u32[]{:S(2)}) collective-permute-start(bf16[64,1024]{1,0:T(8,128)(2,1)S(1)} %get-tuple-element.43), channel_id=1, source_target_pairs={{0,24},{4,28},{8,0},{12,4},{16,8},{20,12},{24,16},{28,20},{32,56},... | collective-permute-start | bytes 393224 | tf_op jit(solution)/shard_map/ppermute | solution.py:284
  191.8 7.4 %collective-permute-start.5 = (bf16[64,1024]{1,0:T(8,128)(2,1)S(1)}, bf16[64,1024]{1,0:T(8,128)(2,1)S(1)}, u32[]{:S(2)}, u32[]{:S(2)}) collective-permute-start(bf16[64,1024]{1,0:T(8,128)(2,1)S(1)} %get-tuple-element.44), channel_id=1, source_target_pairs={{0,16},{4,20},{8,24},{12,28},{16,0},{20,4},{24,8},{28,12},{32,48},... | collective-permute-start | bytes 393224 | tf_op jit(solution)/shard_map/ppermute | solution.py:284
  194.9 6.2 %collective-permute-start.10 = (bf16[64,1024]{1,0:T(8,128)(2,1)S(1)}, bf16[64,1024]{1,0:T(8,128)(2,1)S(1)}, u32[]{:S(2)}, u32[]{:S(2)}) collective-permute-start(bf16[64,1024]{1,0:T(8,128)(2,1)S(1)} %get-tuple-element.39), channel_id=1, source_target_pairs={{0,32},{4,36},{8,40},{12,44},{16,48},{20,52},{24,56},{28,60},{32,6... | collective-permute-start | bytes 393224 | tf_op jit(solution)/shard_map/ppermute | solution.py:284
  195.0 7.1 %collective-permute-start.12 = (bf16[64,1024]{1,0:T(8,128)(2,1)S(1)}, bf16[64,1024]{1,0:T(8,128)(2,1)S(1)}, u32[]{:S(2)}, u32[]{:S(2)}) collective-permute-start(bf16[64,1024]{1,0:T(8,128)(2,1)S(1)} %get-tuple-element.40), channel_id=1, source_target_pairs={{0,96},{4,100},{8,104},{12,108},{16,112},{20,116},{24,120},{28,124... | collective-permute-start | bytes 393224 | tf_op jit(solution)/shard_map/ppermute | solution.py:284
  198.2 6.5 %collective-permute-start.11 = (bf16[64,1024]{1,0:T(8,128)(2,1)S(1)}, bf16[64,1024]{1,0:T(8,128)(2,1)S(1)}, u32[]{:S(2)}, u32[]{:S(2)}) collective-permute-start(bf16[64,1024]{1,0:T(8,128)(2,1)S(1)} %get-tuple-element.41), channel_id=1, source_target_pairs={{0,64},{4,68},{8,72},{12,76},{16,80},{20,84},{24,88},{28,92},{32,9... | collective-permute-start | bytes 393224 | tf_op jit(solution)/shard_map/ppermute | solution.py:284
Sparse Core Ops, SparseCore 0:
  10.9 72.6 all-gather.1
  149.0 44.2 reduce-scatter.1

commit v6 on v4

--- a/solution.py
+++ b/solution.py
@@ -349,6 +349,7 @@
     terms = memory_terms(grad_keys, grad_values, weights)
     other, terms = lax.optimization_barrier((other, terms))
     pieces = home_terms(relative_table(core), memory, grad_keys, grad_values, other)
+    terms, returned, pieces = lax.optimization_barrier((terms, returned, pieces))
     grad_memory = lax.psum_scatter(terms, "fsdp", scatter_dimension=0, tiled=True)
     context, grad_query = unpack_slots(slots, returned)
     sums_y = first_sums(ring_exchange(pieces[:RING], True))

time: 207 us -> 207 us (level)
  waiting for transfers between devices: 84.2 us -> 92.7 us
  starting transfers between devices: 34.4 us -> 26.3 us
    all_to_all x1, waiting for transfers between devices: 0.01 us -> 10.1 us  [per_device(): lax.all_to_all(answers, 'dp', split_axis=0, concat_axis=0, tiled=True)]
    ppermute x12, starting transfers between devices: 21.2 us -> 13.1 us  [ring_exchange(): received.append(lax.ppermute(pieces[step], 'dp', perm))]
where the time goes in v6:
time: 207 us; the launch traced here: 206 us
  waiting for transfers between devices  92.7 us (45%)
  Pallas kernels  45.7 us (22%)
  starting transfers between devices  26.3 us (13%)
  between operations  14.2 us (7%)
  other arithmetic  12.2 us (6%)
  matrix products  10.1 us (5%)
  local copies, waits for them, and re-layouts  4.63 us (2%)
    all_gather x1, waiting for transfers between devices, per_device(): weights = lax.all_gather(stacked, 'dp', axis=0, tiled=True)  57.4 us
    ppermute x12, waiting for transfers between devices, ring_exchange(): received.append(lax.ppermute(pieces[step], 'dp', perm))  25.2 us
    ppermute x12, starting transfers between devices, ring_exchange(): received.append(lax.ppermute(pieces[step], 'dp', perm))  13.1 us
    pallas_call x1, Pallas kernels, attend(): pl.pallas_call(attend_body, grid=(heads, PEERS // BLOCK_PEERS), in_specs=...  11.1 us
    pallas_call x1, Pallas kernels, memory_terms(): pl.pallas_call(memory_body, grid=(model // block,), in_specs=[pl.BlockSpe...  10.6 us
    all_to_all x1, waiting for transfers between devices, per_device(): lax.all_to_all(answers, 'dp', split_axis=0, concat_axis=0, tiled=True)  10.1 us
    dot_general x1, matrix products, dot(): lax.dot_general(left, right, (((left_dim,), (right_dim,)), ((), ())), pre...  10.1 us
    pallas_call x1, Pallas kernels, home_terms(): pl.pallas_call(home_body, grid_spec=pltpu.PrefetchScalarGridSpec(num_scal...  9.22 us
  transfers between devices with their start and end apart: 17, of which 7 were waited for; matrix products, arithmetic and copies ran while one was open for 11% of the time, Pallas kernels for 13%

profile of v6, /device:TPU:0, one launch (start us, length us, event | category | flops | bytes accessed | tf_op | source)
XLA Modules:
  0.0 205.9 jit_solution(15057096796720860624)
XLA Ops:
  7.2 1.7 pad_maximum_fusion.1
  12.0 4.2 %pack_slots.1 = bf16[32,2,32,512]{3,2,1,0:T(8,128)(2,1)} custom-call(s32[1,512]{1,0:T(1,128)} %add_subtract_fusion.slot_ref, bf16[512,512]{1,0:T(8,128)(2,1)} %query_ref.1, bf16[512,512]{1,0:T(8,128)(2,1)} %grad_ref.1), custom_call_target="tpu_custom_call" | custom-call | tf_op jit(solution)/shard_map/pack_slots/pallas_call | solution.py:47
  16.3 7.4 %all-to-all-start = ((bf16[32,2,32,512]{3,2,1,0:T(8,128)(2,1)}), bf16[32,2,32,512]{3,2,1,0:T(8,128)(2,1)S(1)}, u32[]{:S(2)}, u32[]{:S(2)}) async-start(bf16[32,2,32,512]{3,2,1,0:T(8,128)(2,1)} %pack_slots.1), calls=%async_computation | async-start | bytes 4194304 | tf_op jit(solution)/shard_map/all_to_all | solution.py:338
  24.0 1.3 reshape.134.wanted_ref
  26.0 57.4 %all-gather.2.cloned.1.call-done.weight_ref = bf16[4096,1024]{1,0:T(8,128)(2,1)} async-done(((bf16[128,1024]{1,0:T(8,128)(2,1)}), bf16[4096,1024]{1,0:T(8,128)(2,1)}) %all-gather.2.cloned.1.call-update) | async-done | bytes 8388624 | tf_op jit(solution)/shard_map/all_gather | solution.py:334
  83.4 10.1 %fusion.key_ref.value_ref = bf16[512,1024]{1,0:T(8,128)(2,1)} fusion(bf16[512,4096]{1,0:T(8,128)(2,1)} %refs_3_.3, bf16[4096,1024]{1,0:T(8,128)(2,1)} %all-gather.2.cloned.1.call-done.weight_ref), kind=kOutput, calls=%fused_computation.1 | convolution fusion | flops 4295491584 | bytes 13631488 | tf_op jit(solution)/shard_map/dot_general | solution.py:20
  93.5 1.4 copy-done
  94.9 11.1 %attend.1 = (bf16[32,2,32,512]{3,2,1,0:T(8,128)(2,1)}, bf16[512,512]{1,0:T(8,128)(2,1)}, bf16[512,512]{1,0:T(8,128)(2,1)}) custom-call(s32[1024,1]{1,0:T(8,128)} %reshape.134.wanted_ref, s32[1,512]{1,0:T(1,128)} %segment_ref.1, bf16[32,2,32,512]{3,2,1,0:T(8,128)(2,1)} %copy-done, bf16[512,1024]{1,0:T(8,128)(2,1)} %fusion.key_ref.value_ref, ...), custom_call_target="tpu_custom_call" | custom-call | tf_op jit(solution)/shard_map/attend/pallas_call | solution.py:145
  106.0 7.0 %away_terms.1 = bf16[2048,1024]{1,0:T(8,128)(2,1)} custom-call(s32[16]{0:T(128)} %get-tuple-element.66.table_ref, bf16[512,4096]{1,0:T(8,128)(2,1)} %refs_3_.3, bf16[512,4096]{1,0:T(8,128)(2,1)} %refs_3_.3, bf16[512,4096]{1,0:T(8,128)(2,1)} %refs_3_.3, bf16[512,4096]{1,0:T(8,128)(2,1)} %refs_3_.3, bf16[512,512]{1,0:T(8,128)(2,1)} %get-tuple-element.30.refs_4_.grad_key_ref, ...), custom_call_target="tpu_custom_call" | custom-call | tf_op jit(solution)/shard_map/away_terms/pallas_call | solution.py:213
  113.2 5.5 %all-to-all-start.1 = ((bf16[32,2,32,512]{3,2,1,0:T(8,128)(2,1)}), bf16[32,2,32,512]{3,2,1,0:T(8,128)(2,1)S(1)}, u32[]{:S(2)}, u32[]{:S(2)}) async-start(bf16[32,2,32,512]{3,2,1,0:T(8,128)(2,1)} %get-tuple-element.33), calls=%async_computation.1 | async-start | bytes 4194304 | tf_op jit(solution)/shard_map/all_to_all | solution.py:345
  118.8 10.6 %memory_terms.1 = bf16[512,4096]{1,0:T(8,128)(2,1)} custom-call(bf16[512,512]{1,0:T(8,128)(2,1)} %get-tuple-element.30.refs_4_.grad_key_ref, bf16[512,512]{1,0:T(8,128)(2,1)} %get-tuple-element.31.refs_5_.grad_value_ref, bf16[4096,1024]{1,0:T(8,128)(2,1)} %all-gather.2.cloned.1.call-done.weight_ref), custom_call_target="tpu_custom_call" | custom-call | tf_op jit(solution)/shard_map/memory_terms/pallas_call | solution.py:306
  129.3 9.2 %home_terms.1 = (bf16[4,64,1024]{2,1,0:T(8,128)(2,1)}, bf16[4,64,1024]{2,1,0:T(8,128)(2,1)}, bf16[4,64,1024]{2,1,0:T(8,128)(2,1)}, bf16[4,64,1024]{2,1,0:T(8,128...) custom-call(s32[16]{0:T(128)} %get-tuple-element.65.table_ref, ...), custom_call_target="tpu_custom_call" | custom-call | tf_op jit(solution)/shard_map/home_terms/pallas_call | solution.py:255
  138.6 10.1 %all-to-all-done.1.in_ref = bf16[32,2,32,512]{3,2,1,0:T(8,128)(2,1)S(1)} async-done(((bf16[32,2,32,512]{3,2,1,0:T(8,128)(2,1)}), bf16[32,2,32,512]{3,2,1,0:T(8,128)(2,1)S(1)}, u32[]{:S(2)}, u32[]{:S(2)}) %all-to-all-start.1) | async-done | bytes 2097184 | tf_op jit(solution)/shard_map/all_to_all | solution.py:345
  148.8 1.7 collective-permute-start.2
  150.5 1.7 collective-permute-start.3
  152.3 1.4 collective-permute-start.8
  153.7 19.7 %collective-permute-done.1 = bf16[4,64,1024]{2,1,0:T(8,128)(2,1)S(1)} collective-permute-done((bf16[4,64,1024]{2,1,0:T(8,128)(2,1)}, bf16[4,64,1024]{2,1,0:T(8,128)(2,1)S(1)}, u32[]{:S(2)}, u32[]{:S(2)}) %collective-permute-start.1) | collective-permute-done | bytes 524320 | tf_op jit(solution)/shard_map/ppermute | solution.py:284
  175.3 3.6 %unpack_slots.1 = (bf16[512,512]{1,0:T(8,128)(2,1)}, bf16[512,512]{1,0:T(8,128)(2,1)}) custom-call(s32[512,1]{1,0:T(8,128)} %sub.36.slot_ref, bf16[32,2,32,512]{3,2,1,0:T(8,128)(2,1)} %copy-done.1), custom_call_target="tpu_custom_call" | custom-call | tf_op jit(solution)/shard_map/unpack_slots/pallas_call | solution.py:74
  178.9 1.7 fusion.7
  180.6 1.5 collective-permute-start.4
  182.1 2.0 collective-permute-start.6
  185.7 1.6 fusion.11
  187.4 3.2 %collective-permute-start.12 = (bf16[64,1024]{1,0:T(8,128)(2,1)S(1)}, bf16[64,1024]{1,0:T(8,128)(2,1)S(1)}, u32[]{:S(2)}, u32[]{:S(2)}) collective-permute-start(bf16[64,1024]{1,0:T(8,128)(2,1)S(1)} %get-tuple-element.58), channel_id=1, source_target_pairs={{0,96},{4,100},{8,104},{12,108},{16,112},{20,116},{24,120},{28,124... | collective-permute-start | bytes 393224 | tf_op jit(solution)/shard_map/ppermute | solution.py:284
  194.5 2.6 %collective-permute-done.11 = bf16[64,1024]{1,0:T(8,128)(2,1)S(1)} collective-permute-done((bf16[64,1024]{1,0:T(8,128)(2,1)S(1)}, bf16[64,1024]{1,0:T(8,128)(2,1)S(1)}, u32[]{:S(2)}, u32[]{:S(2)}) %collective-permute-start.11) | collective-permute-done | bytes 131104 | tf_op jit(solution)/shard_map/ppermute | solution.py:284
  (52 shorter events, 13.9 us)
Async XLA Ops:
  7.2 16.5 %copy-start.4 = (s32[32,32]{1,0:T(8,128)S(1)}, s32[32,32]{1,0:T(8,128)}, u32[]{:S(2)}) copy-start(s32[32,32]{1,0:T(8,128)} %param.16) | copy-start | bytes 12292
  7.2 16.5 %copy-start.5 = (s32[32,32]{1,0:T(8,128)S(1)}, s32[32,32]{1,0:T(8,128)}, u32[]{:S(2)}) copy-start(s32[32,32]{1,0:T(8,128)} %param.17) | copy-start | bytes 12292
  7.2 76.2 %all-gather.2.cloned.1.call-start = ((), (), s32[]{:S(2)}) async-start(), calls=%async_computation.3 | async-start | bytes 8650752 | tf_op jit(solution)/shard_map/all_gather | solution.py:334
  16.3 77.2 %all-to-all-start = ((bf16[32,2,32,512]{3,2,1,0:T(8,128)(2,1)}), bf16[32,2,32,512]{3,2,1,0:T(8,128)(2,1)S(1)}, u32[]{:S(2)}, u32[]{:S(2)}) async-start(bf16[32,2,32,512]{3,2,1,0:T(8,128)(2,1)} %pack_slots.1), calls=%async_computation | async-start | bytes 4194304 | tf_op jit(solution)/shard_map/all_to_all | solution.py:338
  93.5 1.4 copy-start
  113.0 16.4 %collective-permute-start = (bf16[2048,1024]{1,0:T(8,128)(2,1)}, bf16[2048,1024]{1,0:T(8,128)(2,1)}, u32[]{:S(2)}, u32[]{:S(2)}) collective-permute-start(bf16[2048,1024]{1,0:T(8,128)(2,1)} %away_terms.1), channel_id=1, source_target_pairs={{0,4},{4,0},{8,12},{12,8},{16,20},{20,16},{24,28},{28,24},{32,36},... | collective-permute-start | bytes 12582920 | tf_op jit(solution)/shard_map/ppermute | solution.py:348
  113.2 35.5 %all-to-all-start.1 = ((bf16[32,2,32,512]{3,2,1,0:T(8,128)(2,1)}), bf16[32,2,32,512]{3,2,1,0:T(8,128)(2,1)S(1)}, u32[]{:S(2)}, u32[]{:S(2)}) async-start(bf16[32,2,32,512]{3,2,1,0:T(8,128)(2,1)} %get-tuple-element.33), calls=%async_computation.1 | async-start | bytes 4194304 | tf_op jit(solution)/shard_map/all_to_all | solution.py:345
  118.7 80.4 %reduce-scatter.2.cloned.1.call-start = ((), (), s32[]{:S(2)}) async-start(), calls=%async_computation.4 | async-start | bytes 5242880 | tf_op jit(solution)/shard_map/reduce_scatter | solution.py:353
  148.7 26.6 %copy-start.1 = (bf16[32,2,32,512]{3,2,1,0:T(8,128)(2,1)}, bf16[32,2,32,512]{3,2,1,0:T(8,128)(2,1)S(1)}, u32[]{:S(2)}) copy-start(bf16[32,2,32,512]{3,2,1,0:T(8,128)(2,1)S(1)} %all-to-all-done.1.in_ref) | copy-start | bytes 6291460
  148.7 37.0 %copy-start.2 = (bf16[4,64,1024]{2,1,0:T(8,128)(2,1)S(1)}, bf16[4,64,1024]{2,1,0:T(8,128)(2,1)}, u32[]{:S(2)}) copy-start(bf16[4,64,1024]{2,1,0:T(8,128)(2,1)} %get-tuple-element.50) | copy-start | bytes 1572868
  148.7 24.7 %collective-permute-start.1 = (bf16[4,64,1024]{2,1,0:T(8,128)(2,1)}, bf16[4,64,1024]{2,1,0:T(8,128)(2,1)S(1)}, u32[]{:S(2)}, u32[]{:S(2)}) collective-permute-start(bf16[4,64,1024]{2,1,0:T(8,128)(2,1)} %get-tuple-element.47), channel_id=1, source_target_pairs={{0,32},{4,36},{8,40},{12,44},{16,48},{20,52},{24,56},{28,60},{32,6... | collective-permute-start | bytes 1572872 | tf_op jit(solution)/shard_map/ppermute | solution.py:284
  148.8 30.1 %collective-permute-start.2 = (bf16[4,64,1024]{2,1,0:T(8,128)(2,1)}, bf16[4,64,1024]{2,1,0:T(8,128)(2,1)}, u32[]{:S(2)}, u32[]{:S(2)}) collective-permute-start(bf16[4,64,1024]{2,1,0:T(8,128)(2,1)} %get-tuple-element.48), channel_id=1, source_target_pairs={{0,64},{4,68},{8,72},{12,76},{16,80},{20,84},{24,88},{28,92},{32,9... | collective-permute-start | bytes 1572872 | tf_op jit(solution)/shard_map/ppermute | solution.py:284
  150.5 28.3 %collective-permute-start.3 = (bf16[4,64,1024]{2,1,0:T(8,128)(2,1)}, bf16[4,64,1024]{2,1,0:T(8,128)(2,1)}, u32[]{:S(2)}, u32[]{:S(2)}) collective-permute-start(bf16[4,64,1024]{2,1,0:T(8,128)(2,1)} %get-tuple-element.49), channel_id=1, source_target_pairs={{0,96},{4,100},{8,104},{12,108},{16,112},{20,116},{24,120},{28,124... | collective-permute-start | bytes 1572872 | tf_op jit(solution)/shard_map/ppermute | solution.py:284
  152.3 31.9 %collective-permute-start.7 = (bf16[4,64,1024]{2,1,0:T(8,128)(2,1)}, bf16[4,64,1024]{2,1,0:T(8,128)(2,1)}, u32[]{:S(2)}, u32[]{:S(2)}) collective-permute-start(bf16[4,64,1024]{2,1,0:T(8,128)(2,1)} %get-tuple-element.51), channel_id=1, source_target_pairs={{0,8},{4,12},{8,16},{12,20},{16,24},{20,28},{24,0},{28,4},{32,40},... | collective-permute-start | bytes 1572872 | tf_op jit(solution)/shard_map/ppermute | solution.py:284
  152.3 32.9 %collective-permute-start.8 = (bf16[4,64,1024]{2,1,0:T(8,128)(2,1)}, bf16[4,64,1024]{2,1,0:T(8,128)(2,1)}, u32[]{:S(2)}, u32[]{:S(2)}) collective-permute-start(bf16[4,64,1024]{2,1,0:T(8,128)(2,1)} %get-tuple-element.52), channel_id=1, source_target_pairs={{0,16},{4,20},{8,24},{12,28},{16,0},{20,4},{24,8},{28,12},{32,48},... | collective-permute-start | bytes 1572872 | tf_op jit(solution)/shard_map/ppermute | solution.py:284
  173.4 0.8 copy-start.3
  173.4 12.3 %collective-permute-start.9 = (bf16[4,64,1024]{2,1,0:T(8,128)(2,1)}, bf16[4,64,1024]{2,1,0:T(8,128)(2,1)}, u32[]{:S(2)}, u32[]{:S(2)}) collective-permute-start(bf16[4,64,1024]{2,1,0:T(8,128)(2,1)} %get-tuple-element.53), channel_id=1, source_target_pairs={{0,24},{4,28},{8,0},{12,4},{16,8},{20,12},{24,16},{28,20},{32,56},... | collective-permute-start | bytes 1572872 | tf_op jit(solution)/shard_map/ppermute | solution.py:284
  180.6 10.0 %collective-permute-start.4 = (bf16[64,1024]{1,0:T(8,128)(2,1)S(1)}, bf16[64,1024]{1,0:T(8,128)(2,1)S(1)}, u32[]{:S(2)}, u32[]{:S(2)}) collective-permute-start(bf16[64,1024]{1,0:T(8,128)(2,1)S(1)} %get-tuple-element.60), channel_id=1, source_target_pairs={{0,8},{4,12},{8,16},{12,20},{16,24},{20,28},{24,0},{28,4},{32,40},... | collective-permute-start | bytes 393224 | tf_op jit(solution)/shard_map/ppermute | solution.py:284
  182.1 8.9 %collective-permute-start.6 = (bf16[64,1024]{1,0:T(8,128)(2,1)S(1)}, bf16[64,1024]{1,0:T(8,128)(2,1)S(1)}, u32[]{:S(2)}, u32[]{:S(2)}) collective-permute-start(bf16[64,1024]{1,0:T(8,128)(2,1)S(1)} %get-tuple-element.61), channel_id=1, source_target_pairs={{0,24},{4,28},{8,0},{12,4},{16,8},{20,12},{24,16},{28,20},{32,56},... | collective-permute-start | bytes 393224 | tf_op jit(solution)/shard_map/ppermute | solution.py:284
  184.1 6.8 %collective-permute-start.5 = (bf16[64,1024]{1,0:T(8,128)(2,1)S(1)}, bf16[64,1024]{1,0:T(8,128)(2,1)S(1)}, u32[]{:S(2)}, u32[]{:S(2)}) collective-permute-start(bf16[64,1024]{1,0:T(8,128)(2,1)S(1)} %get-tuple-element.62), channel_id=1, source_target_pairs={{0,16},{4,20},{8,24},{12,28},{16,0},{20,4},{24,8},{28,12},{32,48},... | collective-permute-start | bytes 393224 | tf_op jit(solution)/shard_map/ppermute | solution.py:284
  187.3 6.2 %collective-permute-start.10 = (bf16[64,1024]{1,0:T(8,128)(2,1)S(1)}, bf16[64,1024]{1,0:T(8,128)(2,1)S(1)}, u32[]{:S(2)}, u32[]{:S(2)}) collective-permute-start(bf16[64,1024]{1,0:T(8,128)(2,1)S(1)} %get-tuple-element.57), channel_id=1, source_target_pairs={{0,32},{4,36},{8,40},{12,44},{16,48},{20,52},{24,56},{28,60},{32,6... | collective-permute-start | bytes 393224 | tf_op jit(solution)/shard_map/ppermute | solution.py:284
  187.4 7.1 %collective-permute-start.12 = (bf16[64,1024]{1,0:T(8,128)(2,1)S(1)}, bf16[64,1024]{1,0:T(8,128)(2,1)S(1)}, u32[]{:S(2)}, u32[]{:S(2)}) collective-permute-start(bf16[64,1024]{1,0:T(8,128)(2,1)S(1)} %get-tuple-element.58), channel_id=1, source_target_pairs={{0,96},{4,100},{8,104},{12,108},{16,112},{20,116},{24,120},{28,124... | collective-permute-start | bytes 393224 | tf_op jit(solution)/shard_map/ppermute | solution.py:284
  190.6 6.5 %collective-permute-start.11 = (bf16[64,1024]{1,0:T(8,128)(2,1)S(1)}, bf16[64,1024]{1,0:T(8,128)(2,1)S(1)}, u32[]{:S(2)}, u32[]{:S(2)}) collective-permute-start(bf16[64,1024]{1,0:T(8,128)(2,1)S(1)} %get-tuple-element.59), channel_id=1, source_target_pairs={{0,64},{4,68},{8,72},{12,76},{16,80},{20,84},{24,88},{28,92},{32,9... | collective-permute-start | bytes 393224 | tf_op jit(solution)/shard_map/ppermute | solution.py:284
Sparse Core Ops, SparseCore 0:
  10.9 72.4 all-gather.1
  148.8 44.2 reduce-scatter.1
